TPU v7x, 256 devices: a whole 4x4x8 slice. The times are simulated.
256 devices in a mesh: ctx: 64 (over z, x_hi, y), tp: 4 (over x_lo, core).
Axes of the slice: x: 4 (x_hi: 2, x_lo: 2; x = x_hi * 2 + x_lo), y: 4, z: 8, core: 2. Of those that a mesh axis runs over, the one named last changes fastest.
Arguments:
- hit_features: bfloat16 [24576, 1024], P('ctx', 'tp'), may hold values from -6 to 6
- segment: int32 [24576], P('ctx'), may hold values from 0 to 31, never falling along the last dimension, each value on 1 to 1537 neighbouring positions
- norm1_gain: float32 [1024], replicated, may hold values from 0.1 to 1.9
- w_qkv: bfloat16 [3, 1024, 1024], P(None, None, 'tp'), may hold values from -2 to 2
- w_out: bfloat16 [1024, 1024], P('tp'), may hold values from -0.1875 to 0.1875
- norm2_gain: float32 [1024], replicated, may hold values from 0.1 to 1.9
- w_up: bfloat16 [1024, 4096], P(None, 'tp'), may hold values from -0.1875 to 0.1875
- w_down: bfloat16 [4096, 1024], P('tp'), may hold values from -0.09375 to 0.09375
Outputs:
- layer_out: bfloat16 [24576, 1024], P('ctx', 'tp')
Inputs may be any that keep to these rules, and one draw needn't show every extreme that they name: `segment`: never falls from one hit to the next; every event number below 32 appears; each event holds 1 to 1537 consecutive hits and some event holds exactly 1537.
All inputs are finite; a program needn't handle non-finite values.
Results may differ from a plain program's by a relative error of at most 0.014.
Values may be sent and summed in bfloat16 or wider, within the bound.
No kernel may reach another device: no remote copies, remote signals or barrier semaphores. Data moves between devices by JAX's collectives and lax.ppermute only.
A program may use at most 128 MiB of HBM per device.

v0:
```python
import jax
import jax.numpy as jnp
from jax import lax
from jax.experimental import pallas as pl
from jax.experimental.pallas import tpu as pltpu
from jax.sharding import Mesh, PartitionSpec as P


HEAD_DIM = 64
epsilon = 1e-05
neg_fill = -1e30
AXES = ("z", "xh", "y", "xl", "core")
CTX = ("z", "xh", "y")
TP = ("xl", "core")
SIZES = (8, 2, 4, 2, 2)
TAG_ROWS = 8


def flat(place):
    index = 0
    for size, at in zip(SIZES, place):
        index = index * size + at
    return index


def every_place():
    for index in range(256):
        place = []
        for size in reversed(SIZES):
            place.append(index % size)
            index //= size
        yield tuple(reversed(place))


def send(block, move):
    route = []
    for place in every_place():
        target = move(*place)
        if target is not None:
            route.append((flat(place), flat(target)))
    return lax.ppermute(block, AXES, route)


def to_y(distance):
    return lambda z, xh, y, xl, c: (z, xh, (y + distance) % 4, xl, c)


def to_super(distance):
    def move(z, xh, y, xl, c):
        at = 2 * z + xh + distance
        return (at // 2, at % 2, y, xl, c) if 0 <= at < 16 else None

    return move


def to_core(z, xh, y, xl, c):
    return (z, xh, y, xl, 1 - c)


def to_chip(z, xh, y, xl, c):
    return (z, xh, y, 1 - xl, c)


def params(mib):
    return pltpu.CompilerParams(vmem_limit_bytes=mib << 20)


SMEM = pl.BlockSpec(memory_space=pltpu.SMEM)
VMEM = pl.BlockSpec(memory_space=pltpu.VMEM)
HBM = pl.BlockSpec(memory_space=pltpu.HBM)


def group_orders(x, c):
    return (2 * x + c, 2 * x + 1 - c, 2 * (1 - x) + c, 2 * (1 - x) + 1 - c)


def stage_body(weights, own, segment, weights_out, own_out, tags, sems):
    copies = [
        pltpu.make_async_copy(weights, weights_out, sems.at[0]),
        pltpu.make_async_copy(own, own_out, sems.at[1]),
    ]
    for copy in copies:
        copy.start()
    tag = (segment[...] + 1).astype(jnp.float32)
    tags[...] = jnp.broadcast_to(tag, tags.shape).astype(jnp.bfloat16)
    for copy in copies:
        copy.wait()


def stage(weights, own, segment):
    return pl.pallas_call(
        stage_body,
        name="stage",
        out_shape=[
            jax.ShapeDtypeStruct(weights.shape, weights.dtype),
            jax.ShapeDtypeStruct(own.shape, own.dtype),
            jax.ShapeDtypeStruct((TAG_ROWS, own.shape[0]), jnp.bfloat16),
        ],
        in_specs=[HBM, HBM, VMEM],
        out_specs=[VMEM] * 3,
        scratch_shapes=[pltpu.SemaphoreType.DMA((2,))],
        compiler_params=params(8),
    )(weights, own, segment)


def project_body(place, own, near, far, both, tags, gain, weights, *rest):
    queries, sides, (features, normed, heads) = rest[:4], rest[4:8], rest[8:]
    y = place[0]
    rows = own.shape[0]
    total = jnp.zeros((rows, 1), jnp.float32)
    for source, at in zip((own, near, far, both), group_orders(place[1], place[2])):
        part = source[...].astype(jnp.float32)
        total = total + jnp.sum(part * part, axis=-1, keepdims=True)
        features[at] = source[...]
    scale = lax.rsqrt(total * (1.0 / 1024) + epsilon)
    for j in range(4):
        at = slice(256 * j, 256 * (j + 1))
        normed[:, at] = (features[j].astype(jnp.float32) * scale * gain[:, at]).astype(jnp.bfloat16)
    for c in range(3):
        out = jnp.dot(normed[...], weights[c], preferred_element_type=jnp.float32)
        if c == 0:
            out = out * HEAD_DIM ** (-0.5)
        turned = out.T.astype(jnp.bfloat16)
        for h in range(4):
            heads[h, 64 * c : 64 * (c + 1), :] = turned[64 * h : 64 * (h + 1)]
    for d in range(4):
        h = lax.rem(y + d, 4)
        queries[d][...] = heads[h, 0:64, :]
        sides[d][0:128, :] = heads[h, 64:192, :]
        sides[d][128 : 128 + TAG_ROWS, :] = tags[...]


def project(place, parts, tags, gain, weights):
    rows = parts[0].shape[0]
    return pl.pallas_call(
        project_body,
        name="project",
        out_shape=[jax.ShapeDtypeStruct((64, rows), jnp.bfloat16)] * 4
        + [jax.ShapeDtypeStruct((128 + TAG_ROWS, rows), jnp.bfloat16)] * 4,
        in_specs=[SMEM] + [VMEM] * 7,
        out_specs=[VMEM] * 8,
        scratch_shapes=[
            pltpu.VMEM((4, rows, 256), jnp.bfloat16),
            pltpu.VMEM((rows, 1024), jnp.bfloat16),
            pltpu.VMEM((4, 192, rows), jnp.bfloat16),
        ],
        compiler_params=params(20),
    )(place, *parts, tags, gain, weights)


def pack_body(first, second, third, fourth, out):
    for d, source in enumerate((first, second, third, fourth)):
        out[d] = source[...]


def pack(payloads):
    rows = payloads[0].shape[1]
    return pl.pallas_call(
        pack_body,
        name="pack",
        out_shape=jax.ShapeDtypeStruct((4, 128 + TAG_ROWS, rows), jnp.bfloat16),
        in_specs=[VMEM] * 4,
        out_specs=VMEM,
        compiler_params=params(8),
    )(*payloads)


def attend_body(first, last, *refs):
    queries, own_sides, sides, refs = refs[:4], refs[4], refs[5], refs[6:]
    if not first:
        top_in, mixed_in = refs[:2]
        refs = refs[2:]
    if last:
        outs, refs = refs[:4], refs[4:]
    top, mixed = refs[:2]
    query_tag, key_all, value_all, key_tag, query_low, query_high, key_low, key_high = refs[2:]
    rows = sides.shape[2]
    for i in range(4):
        tag = own_sides[i, 128 : 128 + TAG_ROWS, :].astype(jnp.float32)[0:1]
        query_tag[i] = tag
        query_low[i] = jnp.min(tag)
        query_high[i] = jnp.max(tag)
    all_low = jnp.minimum(jnp.minimum(query_low[0], query_low[1]), jnp.minimum(query_low[2], query_low[3]))
    all_high = jnp.maximum(jnp.maximum(query_high[0], query_high[1]), jnp.maximum(query_high[2], query_high[3]))
    for j in range(4):
        tags = sides[j, 128 : 128 + TAG_ROWS, :].astype(jnp.float32)
        low, high = jnp.min(tags), jnp.max(tags)
        key_low[j] = low
        key_high[j] = high

        @pl.when((all_low <= high) & (low <= all_high))
        def _():
            key_all[j] = sides[j, 0:64, :].astype(jnp.float32).T.astype(jnp.bfloat16)
            value_all[j, 0:64] = sides[j, 64:128, :]
            value_all[j, 64:80] = jnp.ones((16, rows), jnp.bfloat16)
            key_tag[j] = tags.T[:, 0:1]

    if first:
        top[...] = jnp.full(top.shape, neg_fill, jnp.float32)
        mixed[...] = jnp.zeros(mixed.shape, jnp.float32)
    else:
        top[...] = top_in[...]
        mixed[...] = mixed_in[...]

    for i in range(4):

        def pair(j, carry):
            meets = (query_low[i] <= key_high[j]) & (key_low[j] <= query_high[i])

            @pl.when(meets)
            def _():
                scores = jnp.dot(key_all[j], queries[i][...], preferred_element_type=jnp.float32)
                masked = jnp.where(key_tag[j] == query_tag[i], scores, 2 * neg_fill)
                old_top = top[i]
                new_top = jnp.maximum(old_top, jnp.max(masked, axis=0, keepdims=True))
                powered = jnp.exp(masked - new_top).astype(jnp.bfloat16)
                rescale = jnp.exp(old_top - new_top)
                mixed[i] = mixed[i] * rescale + jnp.dot(value_all[j], powered, preferred_element_type=jnp.float32)
                top[i] = new_top

            return carry

        lax.fori_loop(0, 4, pair, 0)
        if last:
            outs[i][...] = (mixed[i, 0:64] / mixed[i, 64:65]).astype(jnp.bfloat16)


def attend(queries, own_sides, sides, state, last):
    rows = queries[0].shape[1]
    first = state is None
    shapes = [(4, 1, rows), (4, 80, rows)]
    args = list(queries) + [own_sides, sides] + ([] if first else list(state))
    scratch = []
    if last:
        out = [jax.ShapeDtypeStruct((64, rows), jnp.bfloat16)] * 4
        scratch = [pltpu.VMEM(s, jnp.float32) for s in shapes]
    else:
        out = [jax.ShapeDtypeStruct(s, jnp.float32) for s in shapes]
    scratch += [
        pltpu.VMEM((4, 1, rows), jnp.float32),
        pltpu.VMEM((4, rows, 64), jnp.bfloat16),
        pltpu.VMEM((4, 80, rows), jnp.bfloat16),
        pltpu.VMEM((4, rows, 1), jnp.float32),
        pltpu.SMEM((4,), jnp.float32),
        pltpu.SMEM((4,), jnp.float32),
        pltpu.SMEM((4,), jnp.float32),
        pltpu.SMEM((4,), jnp.float32),
    ]

    def body(*refs):
        attend_body(first, last, *refs)

    return pl.pallas_call(
        body,
        out_shape=out,
        in_specs=[VMEM] * len(args),
        out_specs=[VMEM] * len(out),
        scratch_shapes=scratch,
        compiler_params=params(16),
    )(*args)


def gather_body(place, first, second, third, fourth, out):
    y = place[0]
    for d, chunk in enumerate((first, second, third, fourth)):
        out[lax.rem(y - d + 4, 4)] = chunk[...]


def gather_heads(place, chunks):
    rows = chunks[0].shape[1]
    return pl.pallas_call(
        gather_body,
        name="gather_heads",
        out_shape=jax.ShapeDtypeStruct((4, 64, rows), jnp.bfloat16),
        in_specs=[SMEM] + [VMEM] * 4,
        out_specs=VMEM,
        compiler_params=params(8),
    )(place, *chunks)


def columns(index):
    return pl.ds(pl.multiple_of(index * 256, 256), 256)


def feed_body(place, *refs):
    parts, mixed, outers, (gain, w_up, w_down), outs, scratch = (
        refs[:4], refs[4:8], refs[8:12], refs[12:15], refs[15:20], refs[20:]
    )
    far_keep, far_give, near_keep, near_give, share = outs
    features, residual, normed = scratch
    x, c = place[1], place[2]
    rows = parts[0].shape[0]
    for source, at in zip(parts, group_orders(x, c)):
        features[at] = source[...]
    attn = jnp.zeros((rows, 1024), jnp.float32)
    for heads, outer in zip(mixed, outers):
        turned = heads[...].reshape(256, rows).astype(jnp.float32).T.astype(jnp.bfloat16)
        attn = attn + jnp.dot(turned, outer[...], preferred_element_type=jnp.float32)
    total = jnp.zeros((rows, 1), jnp.float32)
    for b in range(4):
        part = features[b].astype(jnp.float32) + attn[:, 256 * b : 256 * (b + 1)]
        residual[b] = part
        total = total + jnp.sum(part * part, axis=-1, keepdims=True)
    scale = lax.rsqrt(total * (1.0 / 1024) + epsilon)
    for b in range(4):
        at = slice(256 * b, 256 * (b + 1))
        normed[:, at] = (residual[b] * scale * gain[:, at]).astype(jnp.bfloat16)
    share[...] = residual[2 * x + c]
    raised = jnp.dot(normed[...], w_up[...], preferred_element_type=jnp.float32)
    hidden = (raised * (1.0 + lax.erf(raised * 0.7071067811865476)) * 0.5).astype(jnp.bfloat16)
    near_at, pair_at, far_at, both_at = group_orders(x, c)
    for out, at in ((far_give, both_at), (far_keep, far_at), (near_give, pair_at), (near_keep, near_at)):
        out[...] = jnp.dot(hidden, w_down[:, columns(at)], preferred_element_type=jnp.float32).astype(jnp.bfloat16)


def feed(place, parts, mixed, outers, gain, w_up, w_down):
    rows = parts[0].shape[0]
    return pl.pallas_call(
        feed_body,
        name="feed",
        out_shape=[jax.ShapeDtypeStruct((rows, 256), jnp.bfloat16)] * 4
        + [jax.ShapeDtypeStruct((rows, 256), jnp.float32)],
        in_specs=[SMEM] + [VMEM] * 15,
        out_specs=[VMEM] * 5,
        scratch_shapes=[
            pltpu.VMEM((4, rows, 256), jnp.bfloat16),
            pltpu.VMEM((4, rows, 256), jnp.float32),
            pltpu.VMEM((rows, 1024), jnp.bfloat16),
        ],
        compiler_params=params(32),
    )(place, *parts, *mixed, *outers, gain, w_up, w_down)


def everyone(block):
    far = send(block, to_chip)
    return [block, send(block, to_core), far, send(far, to_core)]


def layer(hit_features, segment, norm1_gain, w_qkv, w_out, norm2_gain, w_up, w_down):
    place = jnp.stack([lax.axis_index("y"), lax.axis_index("xl"), lax.axis_index("core")]).astype(jnp.int32)
    parts = everyone(hit_features)
    weights, parts[0], tags = stage(w_qkv, hit_features, segment[None, :])
    made = project(place, parts, tags, norm1_gain[None, :], weights)
    arrived = [made[4]]
    for d in range(1, 4):
        arrived.append(send(made[4 + d], to_y(d)))
    w_late, _ = lax.optimization_barrier((w_out, made[4]))
    w_far = send(w_late, to_chip)
    sides = pack(arrived)
    lower, upper = send(sides, to_super(1)), send(sides, to_super(-1))
    late = lax.optimization_barrier((*made[1:4], sides))
    queries = [made[0]] + [send(late[d - 1], to_y(d)) for d in range(1, 4)]
    state = attend(queries, sides, sides, None, False)
    w_own, w_far, *state = lax.optimization_barrier((w_late, w_far, *state))
    outers = [w_own, send(w_own, to_core), w_far, send(w_far, to_core)]
    state = attend(queries, sides, lower, state, False)
    mixed = attend(queries, sides, upper, state, True)
    chunks = [mixed[0]] + [None] * 3
    for d in range(1, 4):
        chunks[(4 - d) % 4] = send(mixed[d], to_y(-d))
    heads = everyone(gather_heads(place, chunks))
    far_keep, far_give, near_keep, near_give, share = feed(
        place, parts, heads, outers, norm2_gain[None, :], w_up, w_down
    )
    summed = far_keep.astype(jnp.float32) + send(far_give, to_core).astype(jnp.float32)
    got = send(summed.astype(jnp.bfloat16), to_chip)
    own = share + near_keep.astype(jnp.float32) + send(near_give, to_core).astype(jnp.float32)
    return (own + got.astype(jnp.float32)).astype(jnp.bfloat16)


def solution(mesh):
    fine = Mesh(mesh.devices.reshape(SIZES), AXES)
    return jax.shard_map(
        layer,
        mesh=fine,
        in_specs=(
            P(CTX, TP),
            P(CTX),
            P(),
            P(None, None, TP),
            P(TP, None),
            P(),
            P(None, TP),
            P(TP, None),
        ),
        out_specs=P(CTX, TP),
        check_vma=False,
    )
```

profile of v0, /device:TPU:128, one launch (start us, length us, event | category | flops | bytes accessed | tf_op | source)
XLA Modules:
  0.0 86.7 jit_solution(3917362622572879111)
XLA Ops:
  0.0 1.5 %collective-permute-start.1 = (bf16[384,256]{1,0:T(8,128)(2,1)}, bf16[384,256]{1,0:T(8,128)(2,1)S(1)}, u32[]{:S(2)}, u32[]{:S(2)}) collective-permute-start(bf16[384,256]{1,0:T(8,128)(2,1)} %own.1), channel_id=1, source_target_pairs={{0,2},{1,3},{2,0},{3,1},{4,6},{5,7},{6,4},{7,5},{8,10},{9,11},{10,... | collective-permute-start | bytes 589832 | tf_op jit(solution)/shard_map/ppermute | solution.py:41
  1.5 5.4 %collective-permute-done.1.far.refs_2_ = bf16[384,256]{1,0:T(8,128)(2,1)S(1)} collective-permute-done((bf16[384,256]{1,0:T(8,128)(2,1)}, bf16[384,256]{1,0:T(8,128)(2,1)S(1)}, u32[]{:S(2)}, u32[]{:S(2)}) %collective-permute-start.1) | collective-permute-done | bytes 196640 | tf_op jit(solution)/shard_map/ppermute | solution.py:41
  6.9 0.7 broadcast_in_dim.9.segment
  7.5 1.4 %copy-done.2 = bf16[3,1024,256]{2,1,0:T(8,128)(2,1)S(1)} copy-done((bf16[3,1024,256]{2,1,0:T(8,128)(2,1)S(1)}, bf16[3,1024,256]{2,1,0:T(8,128)(2,1)}, u32[]{:S(2)}) %copy-start.2) | copy-done | bytes 1572888
  9.0 0.9 %copy-done.4 = bf16[384,256]{1,0:T(8,128)(2,1)S(1)} copy-done((bf16[384,256]{1,0:T(8,128)(2,1)S(1)}, bf16[384,256]{1,0:T(8,128)(2,1)}, u32[]{:S(2)}) %copy-start.4) | copy-done | bytes 196632
  10.4 0.7 copy-done.6
  11.0 1.7 %project.1 = (bf16[64,384]{1,0:T(8,128)(2,1)S(1)}, bf16[64,384]{1,0:T(8,128)(2,1)S(1)}, bf16[64,384]{1,0:T(8,128)(2,1)S(1)}, bf16[64,384]{1,0:T(8,128)(2,1)S(1)}...) custom-call(s32[3]{0:T(128)S(1)} %pad_add_fusion.place, ...), custom_call_target="tpu_custom_call" | custom-call | tf_op jit(solution)/shard_map/project/pallas_call | solution.py:135
  12.8 1.6 %collective-permute-start.11 = (bf16[256,1024]{1,0:T(8,128)(2,1)S(1)}, bf16[256,1024]{1,0:T(8,128)(2,1)S(1)}, u32[]{:S(2)}, u32[]{:S(2)}) collective-permute-start(bf16[256,1024]{1,0:T(8,128)(2,1)S(1)} %copy-done.3), channel_id=1, source_target_pairs={{0,2},{1,3},{2,0},{3,1},{4,6},{5,7},{6,4},{7,5},{8,10},{9,11},{10,... | collective-permute-start | bytes 1572872 | tf_op jit(solution)/shard_map/ppermute | solution.py:41
  14.4 1.6 %collective-permute-start.3 = (bf16[136,384]{1,0:T(8,128)(2,1)S(1)}, bf16[136,384]{1,0:T(8,128)(2,1)S(1)}, u32[]{:S(2)}, u32[]{:S(2)}) collective-permute-start(bf16[136,384]{1,0:T(8,128)(2,1)S(1)} %get-tuple-element.45), channel_id=1, source_target_pairs={{0,4},{1,5},{2,6},{3,7},{4,8},{5,9},{6,10},{7,11},{8,12},{9,13},{1... | collective-permute-start | bytes 313352 | tf_op jit(solution)/shard_map/ppermute | solution.py:41
  15.9 2.9 %collective-permute-start.4 = (bf16[136,384]{1,0:T(8,128)(2,1)S(1)}, bf16[136,384]{1,0:T(8,128)(2,1)S(1)}, u32[]{:S(2)}, u32[]{:S(2)}) collective-permute-start(bf16[136,384]{1,0:T(8,128)(2,1)S(1)} %get-tuple-element.46), channel_id=1, source_target_pairs={{0,8},{1,9},{2,10},{3,11},{4,12},{5,13},{6,14},{7,15},{8,0},{9,1},... | collective-permute-start | bytes 313352 | tf_op jit(solution)/shard_map/ppermute | solution.py:41
  18.8 1.3 %collective-permute-start.5 = (bf16[136,384]{1,0:T(8,128)(2,1)S(1)}, bf16[136,384]{1,0:T(8,128)(2,1)S(1)}, u32[]{:S(2)}, u32[]{:S(2)}) collective-permute-start(bf16[136,384]{1,0:T(8,128)(2,1)S(1)} %get-tuple-element.47), channel_id=1, source_target_pairs={{0,12},{1,13},{2,14},{3,15},{4,0},{5,1},{6,2},{7,3},{8,4},{9,5},{1... | collective-permute-start | bytes 313352 | tf_op jit(solution)/shard_map/ppermute | solution.py:41
  20.7 3.4 %collective-permute-done.4.third = bf16[136,384]{1,0:T(8,128)(2,1)S(1)} collective-permute-done((bf16[136,384]{1,0:T(8,128)(2,1)S(1)}, bf16[136,384]{1,0:T(8,128)(2,1)S(1)}, u32[]{:S(2)}, u32[]{:S(2)}) %collective-permute-start.4) | collective-permute-done | bytes 104480 | tf_op jit(solution)/shard_map/ppermute | solution.py:41
  24.2 4.7 %collective-permute-start.10 = (bf16[4,136,384]{2,1,0:T(8,128)(2,1)S(1)}, bf16[4,136,384]{2,1,0:T(8,128)(2,1)S(1)}, u32[]{:S(2)}, u32[]{:S(2)}) collective-permute-start(bf16[4,136,384]{2,1,0:T(8,128)(2,1)S(1)} %pack.1.refs_4_.refs_5_), channel_id=1, source_target_pairs={{0,16},{1,17},{2,18},{3,19},{4,20},{5,21},{6,22},{7,23},{8,24},{9,... | collective-permute-start | bytes 1253384 | tf_op jit(solution)/shard_map/ppermute | solution.py:41
  28.8 4.8 %collective-permute-start.9 = (bf16[4,136,384]{2,1,0:T(8,128)(2,1)S(1)}, bf16[4,136,384]{2,1,0:T(8,128)(2,1)S(1)}, u32[]{:S(2)}, u32[]{:S(2)}) collective-permute-start(bf16[4,136,384]{2,1,0:T(8,128)(2,1)S(1)} %pack.1.refs_4_.refs_5_), channel_id=1, source_target_pairs={{16,0},{17,1},{18,2},{19,3},{20,4},{21,5},{22,6},{23,7},{24,8},{25... | collective-permute-start | bytes 1253384 | tf_op jit(solution)/shard_map/ppermute | solution.py:41
  33.6 1.2 %collective-permute-start.6 = (bf16[64,384]{1,0:T(8,128)(2,1)S(1)}, bf16[64,384]{1,0:T(8,128)(2,1)S(1)}, u32[]{:S(2)}, u32[]{:S(2)}) collective-permute-start(bf16[64,384]{1,0:T(8,128)(2,1)S(1)} %get-tuple-element.48), channel_id=1, source_target_pairs={{0,4},{1,5},{2,6},{3,7},{4,8},{5,9},{6,10},{7,11},{8,12},{9,13},{1... | collective-permute-start | bytes 147464 | tf_op jit(solution)/shard_map/ppermute | solution.py:41
  34.8 2.4 %collective-permute-start.7 = (bf16[64,384]{1,0:T(8,128)(2,1)S(1)}, bf16[64,384]{1,0:T(8,128)(2,1)S(1)}, u32[]{:S(2)}, u32[]{:S(2)}) collective-permute-start(bf16[64,384]{1,0:T(8,128)(2,1)S(1)} %get-tuple-element.49), channel_id=1, source_target_pairs={{0,8},{1,9},{2,10},{3,11},{4,12},{5,13},{6,14},{7,15},{8,0},{9,1},... | collective-permute-start | bytes 147464 | tf_op jit(solution)/shard_map/ppermute | solution.py:41
  37.2 1.8 %collective-permute-done.6.refs_1_ = bf16[64,384]{1,0:T(8,128)(2,1)S(1)} collective-permute-done((bf16[64,384]{1,0:T(8,128)(2,1)S(1)}, bf16[64,384]{1,0:T(8,128)(2,1)S(1)}, u32[]{:S(2)}, u32[]{:S(2)}) %collective-permute-start.6) | collective-permute-done | bytes 49184 | tf_op jit(solution)/shard_map/ppermute | solution.py:41
  39.0 0.9 collective-permute-start.8
  40.4 2.7 %collective-permute-done.8.refs_3_ = bf16[64,384]{1,0:T(8,128)(2,1)S(1)} collective-permute-done((bf16[64,384]{1,0:T(8,128)(2,1)S(1)}, bf16[64,384]{1,0:T(8,128)(2,1)S(1)}, u32[]{:S(2)}, u32[]{:S(2)}) %collective-permute-start.8) | collective-permute-done | bytes 49184 | tf_op jit(solution)/shard_map/ppermute | solution.py:41
  43.1 7.1 %shard_map.82 = (f32[4,1,384]{2,1,0:T(1,128)S(1)}, f32[4,80,384]{2,1,0:T(8,128)S(1)}) custom-call(bf16[64,384]{1,0:T(8,128)(2,1)S(1)} %get-tuple-element.40.refs_0_, bf16[64,384]{1,0:T(8,128)(2,1)S(1)} %collective-permute-done.6.refs_1_, bf16[64,384]{1,0:T(8,128)(2,1)S(1)} %collective-permute-done.7.refs_2_, ...), custom_call_target="tpu_custom_call" | custom-call | tf_op jit(solution)/shard_map/pallas_call | solution.py:253
  50.8 3.4 %shard_map.83 = (f32[4,1,384]{2,1,0:T(1,128)S(1)}, f32[4,80,384]{2,1,0:T(8,128)S(1)}) custom-call(bf16[64,384]{1,0:T(8,128)(2,1)S(1)} %get-tuple-element.40.refs_0_, bf16[64,384]{1,0:T(8,128)(2,1)S(1)} %collective-permute-done.6.refs_1_, bf16[64,384]{1,0:T(8,128)(2,1)S(1)} %collective-permute-done.7.refs_2_, ...), custom_call_target="tpu_custom_call" | custom-call | tf_op jit(solution)/shard_map/pallas_call | solution.py:253
  54.3 4.0 %shard_map.84 = (bf16[64,384]{1,0:T(8,128)(2,1)S(1)}, bf16[64,384]{1,0:T(8,128)(2,1)S(1)}, bf16[64,384]{1,0:T(8,128)(2,1)S(1)}, bf16[64,384]{1,0:T(8,128)(2,1)S(1)}) custom-call(bf16[64,384]{1,0:T(8,128)(2,1)S(1)} %get-tuple-element.40.refs_0_, bf16[64,384]{1,0:T(8,128)(2,1)S(1)} %collective-permute-done.6.refs_1_, ...), custom_call_target="tpu_custom_call" | custom-call | tf_op jit(solution)/shard_map/pallas_call | solution.py:253
  58.5 3.4 %collective-permute-start.13 = (bf16[64,384]{1,0:T(8,128)(2,1)S(1)}, bf16[64,384]{1,0:T(8,128)(2,1)S(1)}, u32[]{:S(2)}, u32[]{:S(2)}) collective-permute-start(bf16[64,384]{1,0:T(8,128)(2,1)S(1)} %get-tuple-element.60), channel_id=1, source_target_pairs={{0,8},{1,9},{2,10},{3,11},{4,12},{5,13},{6,14},{7,15},{8,0},{9,1},... | collective-permute-start | bytes 147464 | tf_op jit(solution)/shard_map/ppermute | solution.py:41
  61.9 0.7 collective-permute-start.14
  62.6 1.5 %collective-permute-done.12.second = bf16[64,384]{1,0:T(8,128)(2,1)S(1)} collective-permute-done((bf16[64,384]{1,0:T(8,128)(2,1)S(1)}, bf16[64,384]{1,0:T(8,128)(2,1)S(1)}, u32[]{:S(2)}, u32[]{:S(2)}) %collective-permute-start.12) | collective-permute-done | bytes 49184 | tf_op jit(solution)/shard_map/ppermute | solution.py:41
  64.7 1.3 %collective-permute-done.14.fourth = bf16[64,384]{1,0:T(8,128)(2,1)S(1)} collective-permute-done((bf16[64,384]{1,0:T(8,128)(2,1)S(1)}, bf16[64,384]{1,0:T(8,128)(2,1)S(1)}, u32[]{:S(2)}, u32[]{:S(2)}) %collective-permute-start.14) | collective-permute-done | bytes 49184 | tf_op jit(solution)/shard_map/ppermute | solution.py:41
  67.2 5.2 %collective-permute-done.16.refs_6_ = bf16[4,64,384]{2,1,0:T(8,128)(2,1)S(1)} collective-permute-done((bf16[4,64,384]{2,1,0:T(8,128)(2,1)S(1)}, bf16[4,64,384]{2,1,0:T(8,128)(2,1)S(1)}, u32[]{:S(2)}, u32[]{:S(2)}) %collective-permute-start.16) | collective-permute-done | bytes 196640 | tf_op jit(solution)/shard_map/ppermute | solution.py:41
  72.4 1.4 %collective-permute-done.17.refs_7_ = bf16[4,64,384]{2,1,0:T(8,128)(2,1)S(1)} collective-permute-done((bf16[4,64,384]{2,1,0:T(8,128)(2,1)S(1)}, bf16[4,64,384]{2,1,0:T(8,128)(2,1)S(1)}, u32[]{:S(2)}, u32[]{:S(2)}) %collective-permute-start.17) | collective-permute-done | bytes 196640 | tf_op jit(solution)/shard_map/ppermute | solution.py:41
  73.8 3.5 %feed.1 = (bf16[384,256]{1,0:T(8,128)(2,1)S(1)}, bf16[384,256]{1,0:T(8,128)(2,1)S(1)}, bf16[384,256]{1,0:T(8,128)(2,1)S(1)}, bf16[384,256]{1,0:T(8,128)(2,1)S(1)}, f32[384,256]{1,0:T(8,128)S(1)}) custom-call(s32[3]{0:T(128)S(1)} %pad_add_fusion.place, bf16[384,256]{1,0:T(8,128)(2,1)S(1)} %get-tuple-element.37.own.refs_0_, ...), custom_call_target="tpu_custom_call" | custom-call | tf_op jit(solution)/shard_map/feed/pallas_call | solution.py:318
  77.9 0.9 %collective-permute-done.21 = bf16[384,256]{1,0:T(8,128)(2,1)S(1)} collective-permute-done((bf16[384,256]{1,0:T(8,128)(2,1)S(1)}, bf16[384,256]{1,0:T(8,128)(2,1)S(1)}, u32[]{:S(2)}, u32[]{:S(2)}) %collective-permute-start.21) | collective-permute-done | bytes 196640 | tf_op jit(solution)/shard_map/ppermute | solution.py:41
  79.5 6.4 %collective-permute-done.22 = bf16[384,256]{1,0:T(8,128)(2,1)S(1)} collective-permute-done((bf16[384,256]{1,0:T(8,128)(2,1)S(1)}, bf16[384,256]{1,0:T(8,128)(2,1)S(1)}, u32[]{:S(2)}, u32[]{:S(2)}) %collective-permute-start.22) | collective-permute-done | bytes 196640 | tf_op jit(solution)/shard_map/ppermute | solution.py:41
  85.9 0.8 add_convert_fusion
  (40 shorter events, 5.4 us)
Async XLA Ops:
  0.0 6.9 %collective-permute-start.1 = (bf16[384,256]{1,0:T(8,128)(2,1)}, bf16[384,256]{1,0:T(8,128)(2,1)S(1)}, u32[]{:S(2)}, u32[]{:S(2)}) collective-permute-start(bf16[384,256]{1,0:T(8,128)(2,1)} %own.1), channel_id=1, source_target_pairs={{0,2},{1,3},{2,0},{3,1},{4,6},{5,7},{6,4},{7,5},{8,10},{9,11},{10,... | collective-permute-start | bytes 589832 | tf_op jit(solution)/shard_map/ppermute | solution.py:41
  1.5 8.9 %collective-permute-start = (bf16[384,256]{1,0:T(8,128)(2,1)}, bf16[384,256]{1,0:T(8,128)(2,1)S(1)}, u32[]{:S(2)}, u32[]{:S(2)}) collective-permute-start(bf16[384,256]{1,0:T(8,128)(2,1)} %own.1), channel_id=1, source_target_pairs={{0,1},{1,0},{2,3},{3,2},{4,5},{5,4},{6,7},{7,6},{8,9},{9,8},{10,11... | collective-permute-start | bytes 589832 | tf_op jit(solution)/shard_map/ppermute | solution.py:41
  6.9 3.5 %collective-permute-start.2 = (bf16[384,256]{1,0:T(8,128)(2,1)S(1)}, bf16[384,256]{1,0:T(8,128)(2,1)S(1)}, u32[]{:S(2)}, u32[]{:S(2)}) collective-permute-start(bf16[384,256]{1,0:T(8,128)(2,1)S(1)} %collective-permute-done.1.far.refs_2_), channel_id=1, source_target_pairs={{0,1},{1,0},{2,3},{3,2},{4,5},{5,4},{6,7},{7,6},{8,9},{9,8},{10,11... | collective-permute-start | bytes 589832 | tf_op jit(solution)/shard_map/ppermute | solution.py:41
  7.5 1.4 %copy-start.2 = (bf16[3,1024,256]{2,1,0:T(8,128)(2,1)S(1)}, bf16[3,1024,256]{2,1,0:T(8,128)(2,1)}, u32[]{:S(2)}) copy-start(bf16[3,1024,256]{2,1,0:T(8,128)(2,1)} %weights.1) | copy-start | bytes 4718596
  8.9 0.9 %copy-start.4 = (bf16[384,256]{1,0:T(8,128)(2,1)S(1)}, bf16[384,256]{1,0:T(8,128)(2,1)}, u32[]{:S(2)}) copy-start(bf16[384,256]{1,0:T(8,128)(2,1)} %own.1) | copy-start | bytes 589828
  9.9 2.9 %copy-start.3 = (bf16[256,1024]{1,0:T(8,128)(2,1)S(1)}, bf16[256,1024]{1,0:T(8,128)(2,1)}, u32[]{:S(2)}) copy-start(bf16[256,1024]{1,0:T(8,128)(2,1)} %refs_8_) | copy-start | bytes 1572868
  10.4 0.7 copy-start.6
  12.8 37.4 %collective-permute-start.11 = (bf16[256,1024]{1,0:T(8,128)(2,1)S(1)}, bf16[256,1024]{1,0:T(8,128)(2,1)S(1)}, u32[]{:S(2)}, u32[]{:S(2)}) collective-permute-start(bf16[256,1024]{1,0:T(8,128)(2,1)S(1)} %copy-done.3), channel_id=1, source_target_pairs={{0,2},{1,3},{2,0},{3,1},{4,6},{5,7},{6,4},{7,5},{8,10},{9,11},{10,... | collective-permute-start | bytes 1572872 | tf_op jit(solution)/shard_map/ppermute | solution.py:41
  14.4 6.3 %collective-permute-start.3 = (bf16[136,384]{1,0:T(8,128)(2,1)S(1)}, bf16[136,384]{1,0:T(8,128)(2,1)S(1)}, u32[]{:S(2)}, u32[]{:S(2)}) collective-permute-start(bf16[136,384]{1,0:T(8,128)(2,1)S(1)} %get-tuple-element.45), channel_id=1, source_target_pairs={{0,4},{1,5},{2,6},{3,7},{4,8},{5,9},{6,10},{7,11},{8,12},{9,13},{1... | collective-permute-start | bytes 313352 | tf_op jit(solution)/shard_map/ppermute | solution.py:41
  15.9 8.2 %collective-permute-start.4 = (bf16[136,384]{1,0:T(8,128)(2,1)S(1)}, bf16[136,384]{1,0:T(8,128)(2,1)S(1)}, u32[]{:S(2)}, u32[]{:S(2)}) collective-permute-start(bf16[136,384]{1,0:T(8,128)(2,1)S(1)} %get-tuple-element.46), channel_id=1, source_target_pairs={{0,8},{1,9},{2,10},{3,11},{4,12},{5,13},{6,14},{7,15},{8,0},{9,1},... | collective-permute-start | bytes 313352 | tf_op jit(solution)/shard_map/ppermute | solution.py:41
  18.8 5.3 %collective-permute-start.5 = (bf16[136,384]{1,0:T(8,128)(2,1)S(1)}, bf16[136,384]{1,0:T(8,128)(2,1)S(1)}, u32[]{:S(2)}, u32[]{:S(2)}) collective-permute-start(bf16[136,384]{1,0:T(8,128)(2,1)S(1)} %get-tuple-element.47), channel_id=1, source_target_pairs={{0,12},{1,13},{2,14},{3,15},{4,0},{5,1},{6,2},{7,3},{8,4},{9,5},{1... | collective-permute-start | bytes 313352 | tf_op jit(solution)/shard_map/ppermute | solution.py:41
  24.2 26.7 %collective-permute-start.10 = (bf16[4,136,384]{2,1,0:T(8,128)(2,1)S(1)}, bf16[4,136,384]{2,1,0:T(8,128)(2,1)S(1)}, u32[]{:S(2)}, u32[]{:S(2)}) collective-permute-start(bf16[4,136,384]{2,1,0:T(8,128)(2,1)S(1)} %pack.1.refs_4_.refs_5_), channel_id=1, source_target_pairs={{0,16},{1,17},{2,18},{3,19},{4,20},{5,21},{6,22},{7,23},{8,24},{9,... | collective-permute-start | bytes 1253384 | tf_op jit(solution)/shard_map/ppermute | solution.py:41
  28.8 25.4 %collective-permute-start.9 = (bf16[4,136,384]{2,1,0:T(8,128)(2,1)S(1)}, bf16[4,136,384]{2,1,0:T(8,128)(2,1)S(1)}, u32[]{:S(2)}, u32[]{:S(2)}) collective-permute-start(bf16[4,136,384]{2,1,0:T(8,128)(2,1)S(1)} %pack.1.refs_4_.refs_5_), channel_id=1, source_target_pairs={{16,0},{17,1},{18,2},{19,3},{20,4},{21,5},{22,6},{23,7},{24,8},{25... | collective-permute-start | bytes 1253384 | tf_op jit(solution)/shard_map/ppermute | solution.py:41
  33.6 5.4 %collective-permute-start.6 = (bf16[64,384]{1,0:T(8,128)(2,1)S(1)}, bf16[64,384]{1,0:T(8,128)(2,1)S(1)}, u32[]{:S(2)}, u32[]{:S(2)}) collective-permute-start(bf16[64,384]{1,0:T(8,128)(2,1)S(1)} %get-tuple-element.48), channel_id=1, source_target_pairs={{0,4},{1,5},{2,6},{3,7},{4,8},{5,9},{6,10},{7,11},{8,12},{9,13},{1... | collective-permute-start | bytes 147464 | tf_op jit(solution)/shard_map/ppermute | solution.py:41
  34.8 5.6 %collective-permute-start.7 = (bf16[64,384]{1,0:T(8,128)(2,1)S(1)}, bf16[64,384]{1,0:T(8,128)(2,1)S(1)}, u32[]{:S(2)}, u32[]{:S(2)}) collective-permute-start(bf16[64,384]{1,0:T(8,128)(2,1)S(1)} %get-tuple-element.49), channel_id=1, source_target_pairs={{0,8},{1,9},{2,10},{3,11},{4,12},{5,13},{6,14},{7,15},{8,0},{9,1},... | collective-permute-start | bytes 147464 | tf_op jit(solution)/shard_map/ppermute | solution.py:41
  39.0 4.1 %collective-permute-start.8 = (bf16[64,384]{1,0:T(8,128)(2,1)S(1)}, bf16[64,384]{1,0:T(8,128)(2,1)S(1)}, u32[]{:S(2)}, u32[]{:S(2)}) collective-permute-start(bf16[64,384]{1,0:T(8,128)(2,1)S(1)} %get-tuple-element.50), channel_id=1, source_target_pairs={{0,12},{1,13},{2,14},{3,15},{4,0},{5,1},{6,2},{7,3},{8,4},{9,5},{1... | collective-permute-start | bytes 147464 | tf_op jit(solution)/shard_map/ppermute | solution.py:41
  43.1 30.7 %copy-start = (bf16[1024,1024]{1,0:T(8,128)(2,1)S(1)}, bf16[1024,1024]{1,0:T(8,128)(2,1)}, u32[]{:S(2)}) copy-start(bf16[1024,1024]{1,0:T(8,128)(2,1)} %refs_13_.1) | copy-start | bytes 6291460
  43.1 30.7 %copy-start.1 = (bf16[1024,1024]{1,0:T(8,128)(2,1)S(1)}, bf16[1024,1024]{1,0:T(8,128)(2,1)}, u32[]{:S(2)}) copy-start(bf16[1024,1024]{1,0:T(8,128)(2,1)} %refs_14_.1) | copy-start | bytes 6291460
  43.1 30.7 %copy-start.5 = (f32[1024]{0:T(1024)S(1)}, f32[1024]{0:T(1024)}, u32[]{:S(2)}) copy-start(f32[1024]{0:T(1024)} %param.13) | copy-start | bytes 12292
  50.2 23.6 %collective-permute-start.18 = (bf16[256,1024]{1,0:T(8,128)(2,1)S(1)}, bf16[256,1024]{1,0:T(8,128)(2,1)S(1)}, u32[]{:S(2)}, u32[]{:S(2)}) collective-permute-start(bf16[256,1024]{1,0:T(8,128)(2,1)S(1)} %copy-done.3), channel_id=1, source_target_pairs={{0,1},{1,0},{2,3},{3,2},{4,5},{5,4},{6,7},{7,6},{8,9},{9,8},{10,11... | collective-permute-start | bytes 1572872 | tf_op jit(solution)/shard_map/ppermute | solution.py:41
  50.3 23.5 %collective-permute-start.19 = (bf16[256,1024]{1,0:T(8,128)(2,1)S(1)}, bf16[256,1024]{1,0:T(8,128)(2,1)S(1)}, u32[]{:S(2)}, u32[]{:S(2)}) collective-permute-start(bf16[256,1024]{1,0:T(8,128)(2,1)S(1)} %collective-permute-done.11.refs_10_), channel_id=1, source_target_pairs={{0,1},{1,0},{2,3},{3,2},{4,5},{5,4},{6,7},{7,6},{8,9},{9,8},{10,11... | collective-permute-start | bytes 1572872 | tf_op jit(solution)/shard_map/ppermute | solution.py:41
  58.3 5.8 %collective-permute-start.12 = (bf16[64,384]{1,0:T(8,128)(2,1)S(1)}, bf16[64,384]{1,0:T(8,128)(2,1)S(1)}, u32[]{:S(2)}, u32[]{:S(2)}) collective-permute-start(bf16[64,384]{1,0:T(8,128)(2,1)S(1)} %get-tuple-element.59), channel_id=1, source_target_pairs={{0,4},{1,5},{2,6},{3,7},{4,8},{5,9},{6,10},{7,11},{8,12},{9,13},{1... | collective-permute-start | bytes 147464 | tf_op jit(solution)/shard_map/ppermute | solution.py:41
  58.5 6.2 %collective-permute-start.13 = (bf16[64,384]{1,0:T(8,128)(2,1)S(1)}, bf16[64,384]{1,0:T(8,128)(2,1)S(1)}, u32[]{:S(2)}, u32[]{:S(2)}) collective-permute-start(bf16[64,384]{1,0:T(8,128)(2,1)S(1)} %get-tuple-element.60), channel_id=1, source_target_pairs={{0,8},{1,9},{2,10},{3,11},{4,12},{5,13},{6,14},{7,15},{8,0},{9,1},... | collective-permute-start | bytes 147464 | tf_op jit(solution)/shard_map/ppermute | solution.py:41
  61.9 4.1 %collective-permute-start.14 = (bf16[64,384]{1,0:T(8,128)(2,1)S(1)}, bf16[64,384]{1,0:T(8,128)(2,1)S(1)}, u32[]{:S(2)}, u32[]{:S(2)}) collective-permute-start(bf16[64,384]{1,0:T(8,128)(2,1)S(1)} %get-tuple-element.61), channel_id=1, source_target_pairs={{0,12},{1,13},{2,14},{3,15},{4,0},{5,1},{6,2},{7,3},{8,4},{9,5},{1... | collective-permute-start | bytes 147464 | tf_op jit(solution)/shard_map/ppermute | solution.py:41
  66.6 5.8 %collective-permute-start.16 = (bf16[4,64,384]{2,1,0:T(8,128)(2,1)S(1)}, bf16[4,64,384]{2,1,0:T(8,128)(2,1)S(1)}, u32[]{:S(2)}, u32[]{:S(2)}) collective-permute-start(bf16[4,64,384]{2,1,0:T(8,128)(2,1)S(1)} %gather_heads.1.refs_4_), channel_id=1, source_target_pairs={{0,2},{1,3},{2,0},{3,1},{4,6},{5,7},{6,4},{7,5},{8,10},{9,11},{10,... | collective-permute-start | bytes 589832 | tf_op jit(solution)/shard_map/ppermute | solution.py:41
  67.2 5.2 %collective-permute-start.15 = (bf16[4,64,384]{2,1,0:T(8,128)(2,1)S(1)}, bf16[4,64,384]{2,1,0:T(8,128)(2,1)S(1)}, u32[]{:S(2)}, u32[]{:S(2)}) collective-permute-start(bf16[4,64,384]{2,1,0:T(8,128)(2,1)S(1)} %gather_heads.1.refs_4_), channel_id=1, source_target_pairs={{0,1},{1,0},{2,3},{3,2},{4,5},{5,4},{6,7},{7,6},{8,9},{9,8},{10,11... | collective-permute-start | bytes 589832 | tf_op jit(solution)/shard_map/ppermute | solution.py:41
  72.3 1.4 %collective-permute-start.17 = (bf16[4,64,384]{2,1,0:T(8,128)(2,1)S(1)}, bf16[4,64,384]{2,1,0:T(8,128)(2,1)S(1)}, u32[]{:S(2)}, u32[]{:S(2)}) collective-permute-start(bf16[4,64,384]{2,1,0:T(8,128)(2,1)S(1)} %collective-permute-done.16.refs_6_), channel_id=1, source_target_pairs={{0,1},{1,0},{2,3},{3,2},{4,5},{5,4},{6,7},{7,6},{8,9},{9,8},{10,11... | collective-permute-start | bytes 589832 | tf_op jit(solution)/shard_map/ppermute | solution.py:41
  77.3 1.5 %collective-permute-start.21 = (bf16[384,256]{1,0:T(8,128)(2,1)S(1)}, bf16[384,256]{1,0:T(8,128)(2,1)S(1)}, u32[]{:S(2)}, u32[]{:S(2)}) collective-permute-start(bf16[384,256]{1,0:T(8,128)(2,1)S(1)} %get-tuple-element.68), channel_id=1, source_target_pairs={{0,1},{1,0},{2,3},{3,2},{4,5},{5,4},{6,7},{7,6},{8,9},{9,8},{10,11... | collective-permute-start | bytes 589832 | tf_op jit(solution)/shard_map/ppermute | solution.py:41
  77.5 2.0 %collective-permute-start.20 = (bf16[384,256]{1,0:T(8,128)(2,1)S(1)}, bf16[384,256]{1,0:T(8,128)(2,1)S(1)}, u32[]{:S(2)}, u32[]{:S(2)}) collective-permute-start(bf16[384,256]{1,0:T(8,128)(2,1)S(1)} %get-tuple-element.66), channel_id=1, source_target_pairs={{0,1},{1,0},{2,3},{3,2},{4,5},{5,4},{6,7},{7,6},{8,9},{9,8},{10,11... | collective-permute-start | bytes 589832 | tf_op jit(solution)/shard_map/ppermute | solution.py:41
  78.9 7.0 %collective-permute-start.22 = (bf16[384,256]{1,0:T(8,128)(2,1)S(1)}, bf16[384,256]{1,0:T(8,128)(2,1)S(1)}, u32[]{:S(2)}, u32[]{:S(2)}) collective-permute-start(bf16[384,256]{1,0:T(8,128)(2,1)S(1)} %add_convert_fusion.1), channel_id=1, source_target_pairs={{0,2},{1,3},{2,0},{3,1},{4,6},{5,7},{6,4},{7,5},{8,10},{9,11},{10,... | collective-permute-start | bytes 589832 | tf_op jit(solution)/shard_map/ppermute | solution.py:41
where the time goes:
time: 86.9 us; the launch traced here: 86.7 us
  waiting for transfers between devices  31.6 us (36%)
  starting transfers between devices  29.6 us (34%)
  Pallas kernels  20.7 us (24%)
  local copies, waits for them, and re-layouts  3.72 us (4%)
  other arithmetic  0.91 us (1%)
    ppermute x23, waiting for transfers between devices, send(): return lax.ppermute(block, AXES, route)  31.6 us
    ppermute x23, starting transfers between devices, send(): return lax.ppermute(block, AXES, route)  29.6 us
    pallas_call x3, Pallas kernels, attend(): pl.pallas_call(body, out_shape=out, in_specs=[VMEM] * len(args), out_spec...  14.5 us
    pallas_call x1, Pallas kernels, feed(): pl.pallas_call(feed_body, name='feed', out_shape=[jax.ShapeDtypeStruct((r...  3.47 us
    unnamed x14, local copies, waits for them, and re-layouts  3.03 us
  transfers between devices with their start and end apart: 23, of which 13 were waited for; matrix products, arithmetic and copies ran while one was open for 1% of the time, Pallas kernels for 18%

commit v1 on v0

--- a/solution.py
+++ b/solution.py
@@ -74,7 +74,7 @@
     return (2 * x + c, 2 * x + 1 - c, 2 * (1 - x) + c, 2 * (1 - x) + 1 - c)
 
 
-def stage_body(weights, own, segment, weights_out, own_out, tags, sems):
+def stage_body(weights, own, segment, gain, weights_out, own_out, tags, gain_out, sems):
     copies = [
         pltpu.make_async_copy(weights, weights_out, sems.at[0]),
         pltpu.make_async_copy(own, own_out, sems.at[1]),
@@ -83,11 +83,12 @@
         copy.start()
     tag = (segment[...] + 1).astype(jnp.float32)
     tags[...] = jnp.broadcast_to(tag, tags.shape).astype(jnp.bfloat16)
+    gain_out[...] = gain[...]
     for copy in copies:
         copy.wait()
 
 
-def stage(weights, own, segment):
+def stage(weights, own, segment, gain):
     return pl.pallas_call(
         stage_body,
         name="stage",
@@ -95,12 +96,13 @@
             jax.ShapeDtypeStruct(weights.shape, weights.dtype),
             jax.ShapeDtypeStruct(own.shape, own.dtype),
             jax.ShapeDtypeStruct((TAG_ROWS, own.shape[0]), jnp.bfloat16),
+            jax.ShapeDtypeStruct(gain.shape, gain.dtype),
         ],
-        in_specs=[HBM, HBM, VMEM],
-        out_specs=[VMEM] * 3,
+        in_specs=[HBM, HBM, VMEM, VMEM],
+        out_specs=[VMEM] * 4,
         scratch_shapes=[pltpu.SemaphoreType.DMA((2,))],
         compiler_params=params(8),
-    )(weights, own, segment)
+    )(weights, own, segment, gain)
 
 
 def project_body(place, own, near, far, both, tags, gain, weights, *rest):
@@ -333,18 +335,19 @@
 
 def everyone(block):
     far = send(block, to_chip)
-    return [block, send(block, to_core), far, send(far, to_core)]
+    both = send(far, to_core)
+    return [block, send(block, to_core), far, both]
 
 
 def layer(hit_features, segment, norm1_gain, w_qkv, w_out, norm2_gain, w_up, w_down):
     place = jnp.stack([lax.axis_index("y"), lax.axis_index("xl"), lax.axis_index("core")]).astype(jnp.int32)
     parts = everyone(hit_features)
-    weights, parts[0], tags = stage(w_qkv, hit_features, segment[None, :])
-    made = project(place, parts, tags, norm1_gain[None, :], weights)
+    weights, parts[0], tags, gain = stage(w_qkv, hit_features, segment[None, :], norm1_gain[None, :])
+    made = project(place, parts, tags, gain, weights)
     arrived = [made[4]]
     for d in range(1, 4):
         arrived.append(send(made[4 + d], to_y(d)))
-    w_late, _ = lax.optimization_barrier((w_out, made[4]))
+    w_late, _ = lax.optimization_barrier((w_out, parts[2]))
     w_far = send(w_late, to_chip)
     sides = pack(arrived)
     lower, upper = send(sides, to_super(1)), send(sides, to_super(-1))

time: 86.9 us -> 87.1 us (level)
  transfers between devices with their start and end apart: 23 -> 23, of which waited for: 13 -> 13; matrix products, arithmetic and copies ran while one was open for 1% -> 1% of each run, Pallas kernels for 18% -> 20%
where the time goes in v1:
time: 87.1 us; the launch traced here: 86.8 us
  waiting for transfers between devices  31.3 us (36%)
  starting transfers between devices  30 us (34%)
  Pallas kernels  20.7 us (24%)
  local copies, waits for them, and re-layouts  3.72 us (4%)
  other arithmetic  0.91 us (1%)
    ppermute x23, waiting for transfers between devices, send(): return lax.ppermute(block, AXES, route)  31.3 us
    ppermute x23, starting transfers between devices, send(): return lax.ppermute(block, AXES, route)  30 us
    pallas_call x3, Pallas kernels, attend(): pl.pallas_call(body, out_shape=out, in_specs=[VMEM] * len(args), out_spec...  14.6 us
    pallas_call x1, Pallas kernels, feed(): pl.pallas_call(feed_body, name='feed', out_shape=[jax.ShapeDtypeStruct((r...  3.47 us
    unnamed x14, local copies, waits for them, and re-layouts  3.03 us
  transfers between devices with their start and end apart: 23, of which 13 were waited for; matrix products, arithmetic and copies ran while one was open for 1% of the time, Pallas kernels for 20%

profile of v1, /device:TPU:128, one launch (start us, length us, event | category | flops | bytes accessed | tf_op | source)
XLA Modules:
  0.0 86.8 jit_solution(15615179512214558901)
XLA Ops:
  0.0 1.5 %collective-permute-start.1 = (bf16[384,256]{1,0:T(8,128)(2,1)}, bf16[384,256]{1,0:T(8,128)(2,1)S(1)}, u32[]{:S(2)}, u32[]{:S(2)}) collective-permute-start(bf16[384,256]{1,0:T(8,128)(2,1)} %own.1), channel_id=1, source_target_pairs={{0,2},{1,3},{2,0},{3,1},{4,6},{5,7},{6,4},{7,5},{8,10},{9,11},{10,... | collective-permute-start | bytes 589832 | tf_op jit(solution)/shard_map/ppermute | solution.py:41
  1.5 5.4 %collective-permute-done.1.far.refs_2_ = bf16[384,256]{1,0:T(8,128)(2,1)S(1)} collective-permute-done((bf16[384,256]{1,0:T(8,128)(2,1)}, bf16[384,256]{1,0:T(8,128)(2,1)S(1)}, u32[]{:S(2)}, u32[]{:S(2)}) %collective-permute-start.1) | collective-permute-done | bytes 196640 | tf_op jit(solution)/shard_map/ppermute | solution.py:41
  6.9 0.7 broadcast_in_dim.9.segment
  7.5 1.4 %copy-done.2 = bf16[3,1024,256]{2,1,0:T(8,128)(2,1)S(1)} copy-done((bf16[3,1024,256]{2,1,0:T(8,128)(2,1)S(1)}, bf16[3,1024,256]{2,1,0:T(8,128)(2,1)}, u32[]{:S(2)}) %copy-start.2) | copy-done | bytes 1572888
  9.0 0.9 %copy-done.4 = bf16[384,256]{1,0:T(8,128)(2,1)S(1)} copy-done((bf16[384,256]{1,0:T(8,128)(2,1)S(1)}, bf16[384,256]{1,0:T(8,128)(2,1)}, u32[]{:S(2)}) %copy-start.4) | copy-done | bytes 196632
  9.9 0.7 copy-done.6
  10.9 1.6 %collective-permute-start.11 = (bf16[256,1024]{1,0:T(8,128)(2,1)}, bf16[256,1024]{1,0:T(8,128)(2,1)S(1)}, u32[]{:S(2)}, u32[]{:S(2)}) collective-permute-start(bf16[256,1024]{1,0:T(8,128)(2,1)} %refs_8_), channel_id=1, source_target_pairs={{0,2},{1,3},{2,0},{3,1},{4,6},{5,7},{6,4},{7,5},{8,10},{9,11},{10,... | collective-permute-start | bytes 1572872 | tf_op jit(solution)/shard_map/ppermute | solution.py:41
  12.6 1.7 %project.1 = (bf16[64,384]{1,0:T(8,128)(2,1)S(1)}, bf16[64,384]{1,0:T(8,128)(2,1)S(1)}, bf16[64,384]{1,0:T(8,128)(2,1)S(1)}, bf16[64,384]{1,0:T(8,128)(2,1)S(1)}...) custom-call(s32[3]{0:T(128)S(1)} %pad_add_fusion.place, ...), custom_call_target="tpu_custom_call" | custom-call | tf_op jit(solution)/shard_map/project/pallas_call | solution.py:137
  14.4 1.7 %collective-permute-start.3 = (bf16[136,384]{1,0:T(8,128)(2,1)S(1)}, bf16[136,384]{1,0:T(8,128)(2,1)S(1)}, u32[]{:S(2)}, u32[]{:S(2)}) collective-permute-start(bf16[136,384]{1,0:T(8,128)(2,1)S(1)} %get-tuple-element.47), channel_id=1, source_target_pairs={{0,4},{1,5},{2,6},{3,7},{4,8},{5,9},{6,10},{7,11},{8,12},{9,13},{1... | collective-permute-start | bytes 313352 | tf_op jit(solution)/shard_map/ppermute | solution.py:41
  16.0 2.9 %collective-permute-start.4 = (bf16[136,384]{1,0:T(8,128)(2,1)S(1)}, bf16[136,384]{1,0:T(8,128)(2,1)S(1)}, u32[]{:S(2)}, u32[]{:S(2)}) collective-permute-start(bf16[136,384]{1,0:T(8,128)(2,1)S(1)} %get-tuple-element.48), channel_id=1, source_target_pairs={{0,8},{1,9},{2,10},{3,11},{4,12},{5,13},{6,14},{7,15},{8,0},{9,1},... | collective-permute-start | bytes 313352 | tf_op jit(solution)/shard_map/ppermute | solution.py:41
  18.9 1.3 %collective-permute-start.5 = (bf16[136,384]{1,0:T(8,128)(2,1)S(1)}, bf16[136,384]{1,0:T(8,128)(2,1)S(1)}, u32[]{:S(2)}, u32[]{:S(2)}) collective-permute-start(bf16[136,384]{1,0:T(8,128)(2,1)S(1)} %get-tuple-element.49), channel_id=1, source_target_pairs={{0,12},{1,13},{2,14},{3,15},{4,0},{5,1},{6,2},{7,3},{8,4},{9,5},{1... | collective-permute-start | bytes 313352 | tf_op jit(solution)/shard_map/ppermute | solution.py:41
  20.8 3.4 %collective-permute-done.4.third = bf16[136,384]{1,0:T(8,128)(2,1)S(1)} collective-permute-done((bf16[136,384]{1,0:T(8,128)(2,1)S(1)}, bf16[136,384]{1,0:T(8,128)(2,1)S(1)}, u32[]{:S(2)}, u32[]{:S(2)}) %collective-permute-start.4) | collective-permute-done | bytes 104480 | tf_op jit(solution)/shard_map/ppermute | solution.py:41
  24.2 4.6 %collective-permute-start.10 = (bf16[4,136,384]{2,1,0:T(8,128)(2,1)S(1)}, bf16[4,136,384]{2,1,0:T(8,128)(2,1)S(1)}, u32[]{:S(2)}, u32[]{:S(2)}) collective-permute-start(bf16[4,136,384]{2,1,0:T(8,128)(2,1)S(1)} %pack.1.refs_4_.refs_5_), channel_id=1, source_target_pairs={{0,16},{1,17},{2,18},{3,19},{4,20},{5,21},{6,22},{7,23},{8,24},{9,... | collective-permute-start | bytes 1253384 | tf_op jit(solution)/shard_map/ppermute | solution.py:41
  28.9 4.8 %collective-permute-start.9 = (bf16[4,136,384]{2,1,0:T(8,128)(2,1)S(1)}, bf16[4,136,384]{2,1,0:T(8,128)(2,1)S(1)}, u32[]{:S(2)}, u32[]{:S(2)}) collective-permute-start(bf16[4,136,384]{2,1,0:T(8,128)(2,1)S(1)} %pack.1.refs_4_.refs_5_), channel_id=1, source_target_pairs={{16,0},{17,1},{18,2},{19,3},{20,4},{21,5},{22,6},{23,7},{24,8},{25... | collective-permute-start | bytes 1253384 | tf_op jit(solution)/shard_map/ppermute | solution.py:41
  33.7 1.3 %collective-permute-start.6 = (bf16[64,384]{1,0:T(8,128)(2,1)S(1)}, bf16[64,384]{1,0:T(8,128)(2,1)S(1)}, u32[]{:S(2)}, u32[]{:S(2)}) collective-permute-start(bf16[64,384]{1,0:T(8,128)(2,1)S(1)} %get-tuple-element.50), channel_id=1, source_target_pairs={{0,4},{1,5},{2,6},{3,7},{4,8},{5,9},{6,10},{7,11},{8,12},{9,13},{1... | collective-permute-start | bytes 147464 | tf_op jit(solution)/shard_map/ppermute | solution.py:41
  35.0 2.4 %collective-permute-start.7 = (bf16[64,384]{1,0:T(8,128)(2,1)S(1)}, bf16[64,384]{1,0:T(8,128)(2,1)S(1)}, u32[]{:S(2)}, u32[]{:S(2)}) collective-permute-start(bf16[64,384]{1,0:T(8,128)(2,1)S(1)} %get-tuple-element.51), channel_id=1, source_target_pairs={{0,8},{1,9},{2,10},{3,11},{4,12},{5,13},{6,14},{7,15},{8,0},{9,1},... | collective-permute-start | bytes 147464 | tf_op jit(solution)/shard_map/ppermute | solution.py:41
  37.4 1.7 %collective-permute-done.6.refs_1_ = bf16[64,384]{1,0:T(8,128)(2,1)S(1)} collective-permute-done((bf16[64,384]{1,0:T(8,128)(2,1)S(1)}, bf16[64,384]{1,0:T(8,128)(2,1)S(1)}, u32[]{:S(2)}, u32[]{:S(2)}) %collective-permute-start.6) | collective-permute-done | bytes 49184 | tf_op jit(solution)/shard_map/ppermute | solution.py:41
  39.1 1.0 %collective-permute-start.8 = (bf16[64,384]{1,0:T(8,128)(2,1)S(1)}, bf16[64,384]{1,0:T(8,128)(2,1)S(1)}, u32[]{:S(2)}, u32[]{:S(2)}) collective-permute-start(bf16[64,384]{1,0:T(8,128)(2,1)S(1)} %get-tuple-element.52), channel_id=1, source_target_pairs={{0,12},{1,13},{2,14},{3,15},{4,0},{5,1},{6,2},{7,3},{8,4},{9,5},{1... | collective-permute-start | bytes 147464 | tf_op jit(solution)/shard_map/ppermute | solution.py:41
  40.6 2.6 %collective-permute-done.8.refs_3_ = bf16[64,384]{1,0:T(8,128)(2,1)S(1)} collective-permute-done((bf16[64,384]{1,0:T(8,128)(2,1)S(1)}, bf16[64,384]{1,0:T(8,128)(2,1)S(1)}, u32[]{:S(2)}, u32[]{:S(2)}) %collective-permute-start.8) | collective-permute-done | bytes 49184 | tf_op jit(solution)/shard_map/ppermute | solution.py:41
  43.2 7.1 %shard_map.82 = (f32[4,1,384]{2,1,0:T(1,128)S(1)}, f32[4,80,384]{2,1,0:T(8,128)S(1)}) custom-call(bf16[64,384]{1,0:T(8,128)(2,1)S(1)} %get-tuple-element.42.refs_0_, bf16[64,384]{1,0:T(8,128)(2,1)S(1)} %collective-permute-done.6.refs_1_, bf16[64,384]{1,0:T(8,128)(2,1)S(1)} %collective-permute-done.7.refs_2_, ...), custom_call_target="tpu_custom_call" | custom-call | tf_op jit(solution)/shard_map/pallas_call | solution.py:255
  50.9 3.4 %shard_map.83 = (f32[4,1,384]{2,1,0:T(1,128)S(1)}, f32[4,80,384]{2,1,0:T(8,128)S(1)}) custom-call(bf16[64,384]{1,0:T(8,128)(2,1)S(1)} %get-tuple-element.42.refs_0_, bf16[64,384]{1,0:T(8,128)(2,1)S(1)} %collective-permute-done.6.refs_1_, bf16[64,384]{1,0:T(8,128)(2,1)S(1)} %collective-permute-done.7.refs_2_, ...), custom_call_target="tpu_custom_call" | custom-call | tf_op jit(solution)/shard_map/pallas_call | solution.py:255
  54.4 4.0 %shard_map.84 = (bf16[64,384]{1,0:T(8,128)(2,1)S(1)}, bf16[64,384]{1,0:T(8,128)(2,1)S(1)}, bf16[64,384]{1,0:T(8,128)(2,1)S(1)}, bf16[64,384]{1,0:T(8,128)(2,1)S(1)}) custom-call(bf16[64,384]{1,0:T(8,128)(2,1)S(1)} %get-tuple-element.42.refs_0_, bf16[64,384]{1,0:T(8,128)(2,1)S(1)} %collective-permute-done.6.refs_1_, ...), custom_call_target="tpu_custom_call" | custom-call | tf_op jit(solution)/shard_map/pallas_call | solution.py:255
  58.8 3.3 %collective-permute-start.13 = (bf16[64,384]{1,0:T(8,128)(2,1)S(1)}, bf16[64,384]{1,0:T(8,128)(2,1)S(1)}, u32[]{:S(2)}, u32[]{:S(2)}) collective-permute-start(bf16[64,384]{1,0:T(8,128)(2,1)S(1)} %get-tuple-element.62), channel_id=1, source_target_pairs={{0,8},{1,9},{2,10},{3,11},{4,12},{5,13},{6,14},{7,15},{8,0},{9,1},... | collective-permute-start | bytes 147464 | tf_op jit(solution)/shard_map/ppermute | solution.py:41
  62.1 0.8 collective-permute-start.14
  62.9 1.4 %collective-permute-done.12.second = bf16[64,384]{1,0:T(8,128)(2,1)S(1)} collective-permute-done((bf16[64,384]{1,0:T(8,128)(2,1)S(1)}, bf16[64,384]{1,0:T(8,128)(2,1)S(1)}, u32[]{:S(2)}, u32[]{:S(2)}) %collective-permute-start.12) | collective-permute-done | bytes 49184 | tf_op jit(solution)/shard_map/ppermute | solution.py:41
  64.9 1.3 %collective-permute-done.14.fourth = bf16[64,384]{1,0:T(8,128)(2,1)S(1)} collective-permute-done((bf16[64,384]{1,0:T(8,128)(2,1)S(1)}, bf16[64,384]{1,0:T(8,128)(2,1)S(1)}, u32[]{:S(2)}, u32[]{:S(2)}) %collective-permute-start.14) | collective-permute-done | bytes 49184 | tf_op jit(solution)/shard_map/ppermute | solution.py:41
  67.4 5.1 %collective-permute-done.16.refs_6_ = bf16[4,64,384]{2,1,0:T(8,128)(2,1)S(1)} collective-permute-done((bf16[4,64,384]{2,1,0:T(8,128)(2,1)S(1)}, bf16[4,64,384]{2,1,0:T(8,128)(2,1)S(1)}, u32[]{:S(2)}, u32[]{:S(2)}) %collective-permute-start.16) | collective-permute-done | bytes 196640 | tf_op jit(solution)/shard_map/ppermute | solution.py:41
  72.5 1.4 %collective-permute-done.17.refs_7_ = bf16[4,64,384]{2,1,0:T(8,128)(2,1)S(1)} collective-permute-done((bf16[4,64,384]{2,1,0:T(8,128)(2,1)S(1)}, bf16[4,64,384]{2,1,0:T(8,128)(2,1)S(1)}, u32[]{:S(2)}, u32[]{:S(2)}) %collective-permute-start.17) | collective-permute-done | bytes 196640 | tf_op jit(solution)/shard_map/ppermute | solution.py:41
  73.9 3.5 %feed.1 = (bf16[384,256]{1,0:T(8,128)(2,1)S(1)}, bf16[384,256]{1,0:T(8,128)(2,1)S(1)}, bf16[384,256]{1,0:T(8,128)(2,1)S(1)}, bf16[384,256]{1,0:T(8,128)(2,1)S(1)}, f32[384,256]{1,0:T(8,128)S(1)}) custom-call(s32[3]{0:T(128)S(1)} %pad_add_fusion.place, bf16[384,256]{1,0:T(8,128)(2,1)S(1)} %get-tuple-element.38.own.refs_0_, ...), custom_call_target="tpu_custom_call" | custom-call | tf_op jit(solution)/shard_map/feed/pallas_call | solution.py:320
  78.0 0.9 %collective-permute-done.21 = bf16[384,256]{1,0:T(8,128)(2,1)S(1)} collective-permute-done((bf16[384,256]{1,0:T(8,128)(2,1)S(1)}, bf16[384,256]{1,0:T(8,128)(2,1)S(1)}, u32[]{:S(2)}, u32[]{:S(2)}) %collective-permute-start.21) | collective-permute-done | bytes 196640 | tf_op jit(solution)/shard_map/ppermute | solution.py:41
  79.6 6.4 %collective-permute-done.22 = bf16[384,256]{1,0:T(8,128)(2,1)S(1)} collective-permute-done((bf16[384,256]{1,0:T(8,128)(2,1)S(1)}, bf16[384,256]{1,0:T(8,128)(2,1)S(1)}, u32[]{:S(2)}, u32[]{:S(2)}) %collective-permute-start.22) | collective-permute-done | bytes 196640 | tf_op jit(solution)/shard_map/ppermute | solution.py:41
  86.1 0.8 add_convert_fusion
  (40 shorter events, 5.6 us)
Async XLA Ops:
  0.0 6.9 %collective-permute-start.1 = (bf16[384,256]{1,0:T(8,128)(2,1)}, bf16[384,256]{1,0:T(8,128)(2,1)S(1)}, u32[]{:S(2)}, u32[]{:S(2)}) collective-permute-start(bf16[384,256]{1,0:T(8,128)(2,1)} %own.1), channel_id=1, source_target_pairs={{0,2},{1,3},{2,0},{3,1},{4,6},{5,7},{6,4},{7,5},{8,10},{9,11},{10,... | collective-permute-start | bytes 589832 | tf_op jit(solution)/shard_map/ppermute | solution.py:41
  1.5 11.1 %collective-permute-start = (bf16[384,256]{1,0:T(8,128)(2,1)}, bf16[384,256]{1,0:T(8,128)(2,1)S(1)}, u32[]{:S(2)}, u32[]{:S(2)}) collective-permute-start(bf16[384,256]{1,0:T(8,128)(2,1)} %own.1), channel_id=1, source_target_pairs={{0,1},{1,0},{2,3},{3,2},{4,5},{5,4},{6,7},{7,6},{8,9},{9,8},{10,11... | collective-permute-start | bytes 589832 | tf_op jit(solution)/shard_map/ppermute | solution.py:41
  6.9 5.8 %collective-permute-start.2 = (bf16[384,256]{1,0:T(8,128)(2,1)S(1)}, bf16[384,256]{1,0:T(8,128)(2,1)S(1)}, u32[]{:S(2)}, u32[]{:S(2)}) collective-permute-start(bf16[384,256]{1,0:T(8,128)(2,1)S(1)} %collective-permute-done.1.far.refs_2_), channel_id=1, source_target_pairs={{0,1},{1,0},{2,3},{3,2},{4,5},{5,4},{6,7},{7,6},{8,9},{9,8},{10,11... | collective-permute-start | bytes 589832 | tf_op jit(solution)/shard_map/ppermute | solution.py:41
  7.5 1.4 %copy-start.2 = (bf16[3,1024,256]{2,1,0:T(8,128)(2,1)S(1)}, bf16[3,1024,256]{2,1,0:T(8,128)(2,1)}, u32[]{:S(2)}) copy-start(bf16[3,1024,256]{2,1,0:T(8,128)(2,1)} %weights.1) | copy-start | bytes 4718596
  8.9 0.9 %copy-start.4 = (bf16[384,256]{1,0:T(8,128)(2,1)S(1)}, bf16[384,256]{1,0:T(8,128)(2,1)}, u32[]{:S(2)}) copy-start(bf16[384,256]{1,0:T(8,128)(2,1)} %own.1) | copy-start | bytes 589828
  9.9 0.7 copy-start.6
  10.9 39.4 %collective-permute-start.11 = (bf16[256,1024]{1,0:T(8,128)(2,1)}, bf16[256,1024]{1,0:T(8,128)(2,1)S(1)}, u32[]{:S(2)}, u32[]{:S(2)}) collective-permute-start(bf16[256,1024]{1,0:T(8,128)(2,1)} %refs_8_), channel_id=1, source_target_pairs={{0,2},{1,3},{2,0},{3,1},{4,6},{5,7},{6,4},{7,5},{8,10},{9,11},{10,... | collective-permute-start | bytes 1572872 | tf_op jit(solution)/shard_map/ppermute | solution.py:41
  12.6 37.7 %copy-start.3 = (bf16[256,1024]{1,0:T(8,128)(2,1)S(1)}, bf16[256,1024]{1,0:T(8,128)(2,1)}, u32[]{:S(2)}) copy-start(bf16[256,1024]{1,0:T(8,128)(2,1)} %refs_8_) | copy-start | bytes 1572868
  14.4 6.4 %collective-permute-start.3 = (bf16[136,384]{1,0:T(8,128)(2,1)S(1)}, bf16[136,384]{1,0:T(8,128)(2,1)S(1)}, u32[]{:S(2)}, u32[]{:S(2)}) collective-permute-start(bf16[136,384]{1,0:T(8,128)(2,1)S(1)} %get-tuple-element.47), channel_id=1, source_target_pairs={{0,4},{1,5},{2,6},{3,7},{4,8},{5,9},{6,10},{7,11},{8,12},{9,13},{1... | collective-permute-start | bytes 313352 | tf_op jit(solution)/shard_map/ppermute | solution.py:41
  16.0 8.2 %collective-permute-start.4 = (bf16[136,384]{1,0:T(8,128)(2,1)S(1)}, bf16[136,384]{1,0:T(8,128)(2,1)S(1)}, u32[]{:S(2)}, u32[]{:S(2)}) collective-permute-start(bf16[136,384]{1,0:T(8,128)(2,1)S(1)} %get-tuple-element.48), channel_id=1, source_target_pairs={{0,8},{1,9},{2,10},{3,11},{4,12},{5,13},{6,14},{7,15},{8,0},{9,1},... | collective-permute-start | bytes 313352 | tf_op jit(solution)/shard_map/ppermute | solution.py:41
  18.9 5.3 %collective-permute-start.5 = (bf16[136,384]{1,0:T(8,128)(2,1)S(1)}, bf16[136,384]{1,0:T(8,128)(2,1)S(1)}, u32[]{:S(2)}, u32[]{:S(2)}) collective-permute-start(bf16[136,384]{1,0:T(8,128)(2,1)S(1)} %get-tuple-element.49), channel_id=1, source_target_pairs={{0,12},{1,13},{2,14},{3,15},{4,0},{5,1},{6,2},{7,3},{8,4},{9,5},{1... | collective-permute-start | bytes 313352 | tf_op jit(solution)/shard_map/ppermute | solution.py:41
  24.2 26.7 %collective-permute-start.10 = (bf16[4,136,384]{2,1,0:T(8,128)(2,1)S(1)}, bf16[4,136,384]{2,1,0:T(8,128)(2,1)S(1)}, u32[]{:S(2)}, u32[]{:S(2)}) collective-permute-start(bf16[4,136,384]{2,1,0:T(8,128)(2,1)S(1)} %pack.1.refs_4_.refs_5_), channel_id=1, source_target_pairs={{0,16},{1,17},{2,18},{3,19},{4,20},{5,21},{6,22},{7,23},{8,24},{9,... | collective-permute-start | bytes 1253384 | tf_op jit(solution)/shard_map/ppermute | solution.py:41
  28.9 25.5 %collective-permute-start.9 = (bf16[4,136,384]{2,1,0:T(8,128)(2,1)S(1)}, bf16[4,136,384]{2,1,0:T(8,128)(2,1)S(1)}, u32[]{:S(2)}, u32[]{:S(2)}) collective-permute-start(bf16[4,136,384]{2,1,0:T(8,128)(2,1)S(1)} %pack.1.refs_4_.refs_5_), channel_id=1, source_target_pairs={{16,0},{17,1},{18,2},{19,3},{20,4},{21,5},{22,6},{23,7},{24,8},{25... | collective-permute-start | bytes 1253384 | tf_op jit(solution)/shard_map/ppermute | solution.py:41
  33.7 5.4 %collective-permute-start.6 = (bf16[64,384]{1,0:T(8,128)(2,1)S(1)}, bf16[64,384]{1,0:T(8,128)(2,1)S(1)}, u32[]{:S(2)}, u32[]{:S(2)}) collective-permute-start(bf16[64,384]{1,0:T(8,128)(2,1)S(1)} %get-tuple-element.50), channel_id=1, source_target_pairs={{0,4},{1,5},{2,6},{3,7},{4,8},{5,9},{6,10},{7,11},{8,12},{9,13},{1... | collective-permute-start | bytes 147464 | tf_op jit(solution)/shard_map/ppermute | solution.py:41
  35.0 5.6 %collective-permute-start.7 = (bf16[64,384]{1,0:T(8,128)(2,1)S(1)}, bf16[64,384]{1,0:T(8,128)(2,1)S(1)}, u32[]{:S(2)}, u32[]{:S(2)}) collective-permute-start(bf16[64,384]{1,0:T(8,128)(2,1)S(1)} %get-tuple-element.51), channel_id=1, source_target_pairs={{0,8},{1,9},{2,10},{3,11},{4,12},{5,13},{6,14},{7,15},{8,0},{9,1},... | collective-permute-start | bytes 147464 | tf_op jit(solution)/shard_map/ppermute | solution.py:41
  39.1 4.1 %collective-permute-start.8 = (bf16[64,384]{1,0:T(8,128)(2,1)S(1)}, bf16[64,384]{1,0:T(8,128)(2,1)S(1)}, u32[]{:S(2)}, u32[]{:S(2)}) collective-permute-start(bf16[64,384]{1,0:T(8,128)(2,1)S(1)} %get-tuple-element.52), channel_id=1, source_target_pairs={{0,12},{1,13},{2,14},{3,15},{4,0},{5,1},{6,2},{7,3},{8,4},{9,5},{1... | collective-permute-start | bytes 147464 | tf_op jit(solution)/shard_map/ppermute | solution.py:41
  43.2 30.8 %copy-start = (bf16[1024,1024]{1,0:T(8,128)(2,1)S(1)}, bf16[1024,1024]{1,0:T(8,128)(2,1)}, u32[]{:S(2)}) copy-start(bf16[1024,1024]{1,0:T(8,128)(2,1)} %refs_13_.1) | copy-start | bytes 6291460
  43.2 30.8 %copy-start.1 = (bf16[1024,1024]{1,0:T(8,128)(2,1)S(1)}, bf16[1024,1024]{1,0:T(8,128)(2,1)}, u32[]{:S(2)}) copy-start(bf16[1024,1024]{1,0:T(8,128)(2,1)} %refs_14_.1) | copy-start | bytes 6291460
  43.2 30.8 %copy-start.5 = (f32[1024]{0:T(1024)S(1)}, f32[1024]{0:T(1024)}, u32[]{:S(2)}) copy-start(f32[1024]{0:T(1024)} %param.13) | copy-start | bytes 12292
  50.3 22.2 %collective-permute-start.18 = (bf16[256,1024]{1,0:T(8,128)(2,1)S(1)}, bf16[256,1024]{1,0:T(8,128)(2,1)S(1)}, u32[]{:S(2)}, u32[]{:S(2)}) collective-permute-start(bf16[256,1024]{1,0:T(8,128)(2,1)S(1)} %copy-done.3), channel_id=1, source_target_pairs={{0,1},{1,0},{2,3},{3,2},{4,5},{5,4},{6,7},{7,6},{8,9},{9,8},{10,11... | collective-permute-start | bytes 1572872 | tf_op jit(solution)/shard_map/ppermute | solution.py:41
  50.4 22.1 %collective-permute-start.19 = (bf16[256,1024]{1,0:T(8,128)(2,1)S(1)}, bf16[256,1024]{1,0:T(8,128)(2,1)S(1)}, u32[]{:S(2)}, u32[]{:S(2)}) collective-permute-start(bf16[256,1024]{1,0:T(8,128)(2,1)S(1)} %collective-permute-done.11.refs_10_), channel_id=1, source_target_pairs={{0,1},{1,0},{2,3},{3,2},{4,5},{5,4},{6,7},{7,6},{8,9},{9,8},{10,11... | collective-permute-start | bytes 1572872 | tf_op jit(solution)/shard_map/ppermute | solution.py:41
  58.4 5.9 %collective-permute-start.12 = (bf16[64,384]{1,0:T(8,128)(2,1)S(1)}, bf16[64,384]{1,0:T(8,128)(2,1)S(1)}, u32[]{:S(2)}, u32[]{:S(2)}) collective-permute-start(bf16[64,384]{1,0:T(8,128)(2,1)S(1)} %get-tuple-element.61), channel_id=1, source_target_pairs={{0,4},{1,5},{2,6},{3,7},{4,8},{5,9},{6,10},{7,11},{8,12},{9,13},{1... | collective-permute-start | bytes 147464 | tf_op jit(solution)/shard_map/ppermute | solution.py:41
  58.8 6.1 %collective-permute-start.13 = (bf16[64,384]{1,0:T(8,128)(2,1)S(1)}, bf16[64,384]{1,0:T(8,128)(2,1)S(1)}, u32[]{:S(2)}, u32[]{:S(2)}) collective-permute-start(bf16[64,384]{1,0:T(8,128)(2,1)S(1)} %get-tuple-element.62), channel_id=1, source_target_pairs={{0,8},{1,9},{2,10},{3,11},{4,12},{5,13},{6,14},{7,15},{8,0},{9,1},... | collective-permute-start | bytes 147464 | tf_op jit(solution)/shard_map/ppermute | solution.py:41
  62.1 4.1 %collective-permute-start.14 = (bf16[64,384]{1,0:T(8,128)(2,1)S(1)}, bf16[64,384]{1,0:T(8,128)(2,1)S(1)}, u32[]{:S(2)}, u32[]{:S(2)}) collective-permute-start(bf16[64,384]{1,0:T(8,128)(2,1)S(1)} %get-tuple-element.63), channel_id=1, source_target_pairs={{0,12},{1,13},{2,14},{3,15},{4,0},{5,1},{6,2},{7,3},{8,4},{9,5},{1... | collective-permute-start | bytes 147464 | tf_op jit(solution)/shard_map/ppermute | solution.py:41
  66.7 5.8 %collective-permute-start.16 = (bf16[4,64,384]{2,1,0:T(8,128)(2,1)S(1)}, bf16[4,64,384]{2,1,0:T(8,128)(2,1)S(1)}, u32[]{:S(2)}, u32[]{:S(2)}) collective-permute-start(bf16[4,64,384]{2,1,0:T(8,128)(2,1)S(1)} %gather_heads.1.refs_4_), channel_id=1, source_target_pairs={{0,2},{1,3},{2,0},{3,1},{4,6},{5,7},{6,4},{7,5},{8,10},{9,11},{10,... | collective-permute-start | bytes 589832 | tf_op jit(solution)/shard_map/ppermute | solution.py:41
  67.4 5.1 %collective-permute-start.15 = (bf16[4,64,384]{2,1,0:T(8,128)(2,1)S(1)}, bf16[4,64,384]{2,1,0:T(8,128)(2,1)S(1)}, u32[]{:S(2)}, u32[]{:S(2)}) collective-permute-start(bf16[4,64,384]{2,1,0:T(8,128)(2,1)S(1)} %gather_heads.1.refs_4_), channel_id=1, source_target_pairs={{0,1},{1,0},{2,3},{3,2},{4,5},{5,4},{6,7},{7,6},{8,9},{9,8},{10,11... | collective-permute-start | bytes 589832 | tf_op jit(solution)/shard_map/ppermute | solution.py:41
  72.5 1.4 %collective-permute-start.17 = (bf16[4,64,384]{2,1,0:T(8,128)(2,1)S(1)}, bf16[4,64,384]{2,1,0:T(8,128)(2,1)S(1)}, u32[]{:S(2)}, u32[]{:S(2)}) collective-permute-start(bf16[4,64,384]{2,1,0:T(8,128)(2,1)S(1)} %collective-permute-done.16.refs_6_), channel_id=1, source_target_pairs={{0,1},{1,0},{2,3},{3,2},{4,5},{5,4},{6,7},{7,6},{8,9},{9,8},{10,11... | collective-permute-start | bytes 589832 | tf_op jit(solution)/shard_map/ppermute | solution.py:41
  77.4 1.5 %collective-permute-start.21 = (bf16[384,256]{1,0:T(8,128)(2,1)S(1)}, bf16[384,256]{1,0:T(8,128)(2,1)S(1)}, u32[]{:S(2)}, u32[]{:S(2)}) collective-permute-start(bf16[384,256]{1,0:T(8,128)(2,1)S(1)} %get-tuple-element.70), channel_id=1, source_target_pairs={{0,1},{1,0},{2,3},{3,2},{4,5},{5,4},{6,7},{7,6},{8,9},{9,8},{10,11... | collective-permute-start | bytes 589832 | tf_op jit(solution)/shard_map/ppermute | solution.py:41
  77.6 2.0 %collective-permute-start.20 = (bf16[384,256]{1,0:T(8,128)(2,1)S(1)}, bf16[384,256]{1,0:T(8,128)(2,1)S(1)}, u32[]{:S(2)}, u32[]{:S(2)}) collective-permute-start(bf16[384,256]{1,0:T(8,128)(2,1)S(1)} %get-tuple-element.68), channel_id=1, source_target_pairs={{0,1},{1,0},{2,3},{3,2},{4,5},{5,4},{6,7},{7,6},{8,9},{9,8},{10,11... | collective-permute-start | bytes 589832 | tf_op jit(solution)/shard_map/ppermute | solution.py:41
  79.0 7.0 %collective-permute-start.22 = (bf16[384,256]{1,0:T(8,128)(2,1)S(1)}, bf16[384,256]{1,0:T(8,128)(2,1)S(1)}, u32[]{:S(2)}, u32[]{:S(2)}) collective-permute-start(bf16[384,256]{1,0:T(8,128)(2,1)S(1)} %add_convert_fusion.1), channel_id=1, source_target_pairs={{0,2},{1,3},{2,0},{3,1},{4,6},{5,7},{6,4},{7,5},{8,10},{9,11},{10,... | collective-permute-start | bytes 589832 | tf_op jit(solution)/shard_map/ppermute | solution.py:41

commit v2 on v1

--- a/solution.py
+++ b/solution.py
@@ -106,7 +106,7 @@
 
 
 def project_body(place, own, near, far, both, tags, gain, weights, *rest):
-    queries, sides, (features, normed, heads) = rest[:4], rest[4:8], rest[8:]
+    outs, (features, normed, heads) = rest[:4], rest[4:]
     y = place[0]
     rows = own.shape[0]
     total = jnp.zeros((rows, 1), jnp.float32)
@@ -127,9 +127,8 @@
             heads[h, 64 * c : 64 * (c + 1), :] = turned[64 * h : 64 * (h + 1)]
     for d in range(4):
         h = lax.rem(y + d, 4)
-        queries[d][...] = heads[h, 0:64, :]
-        sides[d][0:128, :] = heads[h, 64:192, :]
-        sides[d][128 : 128 + TAG_ROWS, :] = tags[...]
+        outs[d][0:192, :] = heads[h]
+        outs[d][192 : 192 + TAG_ROWS, :] = tags[...]
 
 
 def project(place, parts, tags, gain, weights):
@@ -137,10 +136,9 @@
     return pl.pallas_call(
         project_body,
         name="project",
-        out_shape=[jax.ShapeDtypeStruct((64, rows), jnp.bfloat16)] * 4
-        + [jax.ShapeDtypeStruct((128 + TAG_ROWS, rows), jnp.bfloat16)] * 4,
+        out_shape=[jax.ShapeDtypeStruct((192 + TAG_ROWS, rows), jnp.bfloat16)] * 4,
         in_specs=[SMEM] + [VMEM] * 7,
-        out_specs=[VMEM] * 8,
+        out_specs=[VMEM] * 4,
         scratch_shapes=[
             pltpu.VMEM((4, rows, 256), jnp.bfloat16),
             pltpu.VMEM((rows, 1024), jnp.bfloat16),
@@ -150,9 +148,10 @@
     )(place, *parts, tags, gain, weights)
 
 
-def pack_body(first, second, third, fourth, out):
+def pack_body(first, second, third, fourth, queries, sides):
     for d, source in enumerate((first, second, third, fourth)):
-        out[d] = source[...]
+        queries[d] = source[0:64, :]
+        sides[d] = source[64 : 192 + TAG_ROWS, :]
 
 
 def pack(payloads):
@@ -160,15 +159,18 @@
     return pl.pallas_call(
         pack_body,
         name="pack",
-        out_shape=jax.ShapeDtypeStruct((4, 128 + TAG_ROWS, rows), jnp.bfloat16),
+        out_shape=[
+            jax.ShapeDtypeStruct((4, 64, rows), jnp.bfloat16),
+            jax.ShapeDtypeStruct((4, 128 + TAG_ROWS, rows), jnp.bfloat16),
+        ],
         in_specs=[VMEM] * 4,
-        out_specs=VMEM,
+        out_specs=[VMEM] * 2,
         compiler_params=params(8),
     )(*payloads)
 
 
 def attend_body(first, last, *refs):
-    queries, own_sides, sides, refs = refs[:4], refs[4], refs[5], refs[6:]
+    queries, own_sides, sides, refs = refs[0], refs[1], refs[2], refs[3:]
     if not first:
         top_in, mixed_in = refs[:2]
         refs = refs[2:]
@@ -211,7 +213,7 @@
 
             @pl.when(meets)
             def _():
-                scores = jnp.dot(key_all[j], queries[i][...], preferred_element_type=jnp.float32)
+                scores = jnp.dot(key_all[j], queries[i], preferred_element_type=jnp.float32)
                 masked = jnp.where(key_tag[j] == query_tag[i], scores, 2 * neg_fill)
                 old_top = top[i]
                 new_top = jnp.maximum(old_top, jnp.max(masked, axis=0, keepdims=True))
@@ -228,10 +230,10 @@
 
 
 def attend(queries, own_sides, sides, state, last):
-    rows = queries[0].shape[1]
+    rows = sides.shape[2]
     first = state is None
     shapes = [(4, 1, rows), (4, 80, rows)]
-    args = list(queries) + [own_sides, sides] + ([] if first else list(state))
+    args = [queries, own_sides, sides] + ([] if first else list(state))
     scratch = []
     if last:
         out = [jax.ShapeDtypeStruct((64, rows), jnp.bfloat16)] * 4
@@ -344,24 +346,22 @@
     parts = everyone(hit_features)
     weights, parts[0], tags, gain = stage(w_qkv, hit_features, segment[None, :], norm1_gain[None, :])
     made = project(place, parts, tags, gain, weights)
-    arrived = [made[4]]
+    arrived = [made[0]]
     for d in range(1, 4):
-        arrived.append(send(made[4 + d], to_y(d)))
+        arrived.append(send(made[d], to_y(d)))
     w_late, _ = lax.optimization_barrier((w_out, parts[2]))
     w_far = send(w_late, to_chip)
-    sides = pack(arrived)
+    queries, sides = pack(arrived)
     lower, upper = send(sides, to_super(1)), send(sides, to_super(-1))
-    late = lax.optimization_barrier((*made[1:4], sides))
-    queries = [made[0]] + [send(late[d - 1], to_y(d)) for d in range(1, 4)]
     state = attend(queries, sides, sides, None, False)
-    w_own, w_far, *state = lax.optimization_barrier((w_late, w_far, *state))
-    outers = [w_own, send(w_own, to_core), w_far, send(w_far, to_core)]
     state = attend(queries, sides, lower, state, False)
     mixed = attend(queries, sides, upper, state, True)
     chunks = [mixed[0]] + [None] * 3
     for d in range(1, 4):
         chunks[(4 - d) % 4] = send(mixed[d], to_y(-d))
-    heads = everyone(gather_heads(place, chunks))
+    gathered, w_own, w_far = lax.optimization_barrier((gather_heads(place, chunks), w_late, w_far))
+    heads = everyone(gathered)
+    outers = [w_own, send(w_own, to_core), w_far, send(w_far, to_core)]
     far_keep, far_give, near_keep, near_give, share = feed(
         place, parts, heads, outers, norm2_gain[None, :], w_up, w_down
     )

time: 87.1 us -> 87.6 us (level)
  the two profiles are of different devices: /device:TPU:128 before, /device:TPU:132 now
where the time goes in v2:
time: 87.6 us; the launch traced here: 87.4 us
  waiting for transfers between devices  38.2 us (44%)
  starting transfers between devices  22.9 us (26%)
  Pallas kernels  21.4 us (24%)
  local copies, waits for them, and re-layouts  3.73 us (4%)
  other arithmetic  0.91 us (1%)
    ppermute x20, waiting for transfers between devices, send(): return lax.ppermute(block, AXES, route)  38.2 us
    ppermute x20, starting transfers between devices, send(): return lax.ppermute(block, AXES, route)  22.9 us
    pallas_call x3, Pallas kernels, attend(): pl.pallas_call(body, out_shape=out, in_specs=[VMEM] * len(args), out_spec...  15.2 us
    pallas_call x1, Pallas kernels, feed(): pl.pallas_call(feed_body, name='feed', out_shape=[jax.ShapeDtypeStruct((r...  3.46 us
    unnamed x14, local copies, waits for them, and re-layouts  3.04 us
  transfers between devices with their start and end apart: 20, of which 11 were waited for; matrix products, arithmetic and copies ran while one was open for 1% of the time, Pallas kernels for 19%

profile of v2, /device:TPU:132, one launch (start us, length us, event | category | flops | bytes accessed | tf_op | source)
XLA Modules:
  0.0 87.4 jit_solution(15292107041105272789)
XLA Ops:
  0.0 1.2 %collective-permute-start.1 = (bf16[384,256]{1,0:T(8,128)(2,1)}, bf16[384,256]{1,0:T(8,128)(2,1)S(1)}, u32[]{:S(2)}, u32[]{:S(2)}) collective-permute-start(bf16[384,256]{1,0:T(8,128)(2,1)} %own.1), channel_id=1, source_target_pairs={{0,2},{1,3},{2,0},{3,1},{4,6},{5,7},{6,4},{7,5},{8,10},{9,11},{10,... | collective-permute-start | bytes 589832 | tf_op jit(solution)/shard_map/ppermute | solution.py:41
  1.2 5.7 %collective-permute-done.1.far.refs_2_ = bf16[384,256]{1,0:T(8,128)(2,1)S(1)} collective-permute-done((bf16[384,256]{1,0:T(8,128)(2,1)}, bf16[384,256]{1,0:T(8,128)(2,1)S(1)}, u32[]{:S(2)}, u32[]{:S(2)}) %collective-permute-start.1) | collective-permute-done | bytes 196640 | tf_op jit(solution)/shard_map/ppermute | solution.py:41
  6.9 0.7 broadcast_in_dim.9.segment
  7.5 1.4 %copy-done.2 = bf16[3,1024,256]{2,1,0:T(8,128)(2,1)S(1)} copy-done((bf16[3,1024,256]{2,1,0:T(8,128)(2,1)S(1)}, bf16[3,1024,256]{2,1,0:T(8,128)(2,1)}, u32[]{:S(2)}) %copy-start.2) | copy-done | bytes 1572888
  9.0 0.9 %copy-done.4 = bf16[384,256]{1,0:T(8,128)(2,1)S(1)} copy-done((bf16[384,256]{1,0:T(8,128)(2,1)S(1)}, bf16[384,256]{1,0:T(8,128)(2,1)}, u32[]{:S(2)}) %copy-start.4) | copy-done | bytes 196632
  9.9 0.7 copy-done.6
  11.0 1.7 %project.1 = (bf16[200,384]{1,0:T(8,128)(2,1)S(1)}, bf16[200,384]{1,0:T(8,128)(2,1)S(1)}, bf16[200,384]{1,0:T(8,128)(2,1)S(1)}, bf16[200,384]{1,0:T(8,128)(2,1)S(1)}) custom-call(s32[3]{0:T(128)S(1)} %pad_add_fusion.place, bf16[384,256]{1,0:T(8,128)(2,1)S(1)} %get-tuple-element.32.own.refs_0_, bf16[384,256]{1,0:T(8,128)(2,1)S(1)} %collective-permute-done.near.refs_1_, ...), custom_call_target="tpu_custom_call" | custom-call | tf_op jit(solution)/shard_map/project/pallas_call | solution.py:136
  12.8 1.7 %collective-permute-start.3 = (bf16[200,384]{1,0:T(8,128)(2,1)S(1)}, bf16[200,384]{1,0:T(8,128)(2,1)S(1)}, u32[]{:S(2)}, u32[]{:S(2)}) collective-permute-start(bf16[200,384]{1,0:T(8,128)(2,1)S(1)} %get-tuple-element.37), channel_id=1, source_target_pairs={{0,4},{1,5},{2,6},{3,7},{4,8},{5,9},{6,10},{7,11},{8,12},{9,13},{1... | collective-permute-start | bytes 460808 | tf_op jit(solution)/shard_map/ppermute | solution.py:41
  14.4 2.9 %collective-permute-start.4 = (bf16[200,384]{1,0:T(8,128)(2,1)S(1)}, bf16[200,384]{1,0:T(8,128)(2,1)S(1)}, u32[]{:S(2)}, u32[]{:S(2)}) collective-permute-start(bf16[200,384]{1,0:T(8,128)(2,1)S(1)} %get-tuple-element.38), channel_id=1, source_target_pairs={{0,8},{1,9},{2,10},{3,11},{4,12},{5,13},{6,14},{7,15},{8,0},{9,1},... | collective-permute-start | bytes 460808 | tf_op jit(solution)/shard_map/ppermute | solution.py:41
  17.3 1.3 %collective-permute-start.5 = (bf16[200,384]{1,0:T(8,128)(2,1)S(1)}, bf16[200,384]{1,0:T(8,128)(2,1)S(1)}, u32[]{:S(2)}, u32[]{:S(2)}) collective-permute-start(bf16[200,384]{1,0:T(8,128)(2,1)S(1)} %get-tuple-element.39), channel_id=1, source_target_pairs={{0,12},{1,13},{2,14},{3,15},{4,0},{5,1},{6,2},{7,3},{8,4},{9,5},{1... | collective-permute-start | bytes 460808 | tf_op jit(solution)/shard_map/ppermute | solution.py:41
  18.7 1.2 %collective-permute-start.11 = (bf16[256,1024]{1,0:T(8,128)(2,1)S(1)}, bf16[256,1024]{1,0:T(8,128)(2,1)S(1)}, u32[]{:S(2)}, u32[]{:S(2)}) collective-permute-start(bf16[256,1024]{1,0:T(8,128)(2,1)S(1)} %copy-done.3), channel_id=1, source_target_pairs={{0,2},{1,3},{2,0},{3,1},{4,6},{5,7},{6,4},{7,5},{8,10},{9,11},{10,... | collective-permute-start | bytes 1572872 | tf_op jit(solution)/shard_map/ppermute | solution.py:41
  19.9 0.6 collective-permute-done.3.second
  20.5 4.5 %collective-permute-done.4.third = bf16[200,384]{1,0:T(8,128)(2,1)S(1)} collective-permute-done((bf16[200,384]{1,0:T(8,128)(2,1)S(1)}, bf16[200,384]{1,0:T(8,128)(2,1)S(1)}, u32[]{:S(2)}, u32[]{:S(2)}) %collective-permute-start.4) | collective-permute-done | bytes 153632 | tf_op jit(solution)/shard_map/ppermute | solution.py:41
  25.1 2.9 %collective-permute-start.7 = (bf16[4,136,384]{2,1,0:T(8,128)(2,1)S(1)}, bf16[4,136,384]{2,1,0:T(8,128)(2,1)S(1)}, u32[]{:S(2)}, u32[]{:S(2)}) collective-permute-start(bf16[4,136,384]{2,1,0:T(8,128)(2,1)S(1)} %get-tuple-element.41.refs_1_.refs_2_), channel_id=1, source_target_pairs={{0,16},{1,17},{2,18},{3,19},{4,20},{5,21},{6,22},{7,23},{8,24},{9,... | collective-permute-start | bytes 1253384 | tf_op jit(solution)/shard_map/ppermute | solution.py:41
  27.9 4.5 %collective-permute-start.6 = (bf16[4,136,384]{2,1,0:T(8,128)(2,1)S(1)}, bf16[4,136,384]{2,1,0:T(8,128)(2,1)S(1)}, u32[]{:S(2)}, u32[]{:S(2)}) collective-permute-start(bf16[4,136,384]{2,1,0:T(8,128)(2,1)S(1)} %get-tuple-element.41.refs_1_.refs_2_), channel_id=1, source_target_pairs={{16,0},{17,1},{18,2},{19,3},{20,4},{21,5},{22,6},{23,7},{24,8},{25... | collective-permute-start | bytes 1253384 | tf_op jit(solution)/shard_map/ppermute | solution.py:41
  32.5 7.1 %shard_map.82 = (f32[4,1,384]{2,1,0:T(1,128)S(1)}, f32[4,80,384]{2,1,0:T(8,128)S(1)}) custom-call(bf16[4,64,384]{2,1,0:T(8,128)(2,1)S(1)} %get-tuple-element.40.refs_0_, bf16[4,136,384]{2,1,0:T(8,128)(2,1)S(1)} %get-tuple-element.41.refs_1_.refs_2_, bf16[4,136,384]{2,1,0:T(8,128)(2,1)S(1)} %get-tuple-element.41.refs_1_.refs_2_), custom_call_target="tpu_custom_call" | custom-call | tf_op jit(solution)/shard_map/pallas_call | solution.py:257
  39.6 10.5 %collective-permute-done.7.refs_2_ = bf16[4,136,384]{2,1,0:T(8,128)(2,1)S(1)} collective-permute-done((bf16[4,136,384]{2,1,0:T(8,128)(2,1)S(1)}, bf16[4,136,384]{2,1,0:T(8,128)(2,1)S(1)}, u32[]{:S(2)}, u32[]{:S(2)}) %collective-permute-start.7) | collective-permute-done | bytes 417824 | tf_op jit(solution)/shard_map/ppermute | solution.py:41
  50.1 4.1 %shard_map.83 = (f32[4,1,384]{2,1,0:T(1,128)S(1)}, f32[4,80,384]{2,1,0:T(8,128)S(1)}) custom-call(bf16[4,64,384]{2,1,0:T(8,128)(2,1)S(1)} %get-tuple-element.40.refs_0_, bf16[4,136,384]{2,1,0:T(8,128)(2,1)S(1)} %get-tuple-element.41.refs_1_.refs_2_, bf16[4,136,384]{2,1,0:T(8,128)(2,1)S(1)} %collective-permute-done.7.refs_2_, ...), custom_call_target="tpu_custom_call" | custom-call | tf_op jit(solution)/shard_map/pallas_call | solution.py:257
  54.2 4.0 %shard_map.84 = (bf16[64,384]{1,0:T(8,128)(2,1)S(1)}, bf16[64,384]{1,0:T(8,128)(2,1)S(1)}, bf16[64,384]{1,0:T(8,128)(2,1)S(1)}, bf16[64,384]{1,0:T(8,128)(2,1)S(1)}) custom-call(bf16[4,64,384]{2,1,0:T(8,128)(2,1)S(1)} %get-tuple-element.40.refs_0_, bf16[4,136,384]{2,1,0:T(8,128)(2,1)S(1)} %get-tuple-element.41.refs_1_.refs_2_, ...), custom_call_target="tpu_custom_call" | custom-call | tf_op jit(solution)/shard_map/pallas_call | solution.py:257
  58.2 0.8 collective-permute-start.8
  58.9 1.9 %collective-permute-start.9 = (bf16[64,384]{1,0:T(8,128)(2,1)S(1)}, bf16[64,384]{1,0:T(8,128)(2,1)S(1)}, u32[]{:S(2)}, u32[]{:S(2)}) collective-permute-start(bf16[64,384]{1,0:T(8,128)(2,1)S(1)} %get-tuple-element.48), channel_id=1, source_target_pairs={{0,8},{1,9},{2,10},{3,11},{4,12},{5,13},{6,14},{7,15},{8,0},{9,1},... | collective-permute-start | bytes 147464 | tf_op jit(solution)/shard_map/ppermute | solution.py:41
  60.8 1.1 %collective-permute-start.10 = (bf16[64,384]{1,0:T(8,128)(2,1)S(1)}, bf16[64,384]{1,0:T(8,128)(2,1)S(1)}, u32[]{:S(2)}, u32[]{:S(2)}) collective-permute-start(bf16[64,384]{1,0:T(8,128)(2,1)S(1)} %get-tuple-element.49), channel_id=1, source_target_pairs={{0,12},{1,13},{2,14},{3,15},{4,0},{5,1},{6,2},{7,3},{8,4},{9,5},{1... | collective-permute-start | bytes 147464 | tf_op jit(solution)/shard_map/ppermute | solution.py:41
  61.9 1.7 %collective-permute-done.8.second = bf16[64,384]{1,0:T(8,128)(2,1)S(1)} collective-permute-done((bf16[64,384]{1,0:T(8,128)(2,1)S(1)}, bf16[64,384]{1,0:T(8,128)(2,1)S(1)}, u32[]{:S(2)}, u32[]{:S(2)}) %collective-permute-start.8) | collective-permute-done | bytes 49184 | tf_op jit(solution)/shard_map/ppermute | solution.py:41
  63.6 1.0 %collective-permute-done.9.third = bf16[64,384]{1,0:T(8,128)(2,1)S(1)} collective-permute-done((bf16[64,384]{1,0:T(8,128)(2,1)S(1)}, bf16[64,384]{1,0:T(8,128)(2,1)S(1)}, u32[]{:S(2)}, u32[]{:S(2)}) %collective-permute-start.9) | collective-permute-done | bytes 49184 | tf_op jit(solution)/shard_map/ppermute | solution.py:41
  66.1 1.1 %collective-permute-start.13 = (bf16[4,64,384]{2,1,0:T(8,128)(2,1)S(1)}, bf16[4,64,384]{2,1,0:T(8,128)(2,1)S(1)}, u32[]{:S(2)}, u32[]{:S(2)}) collective-permute-start(bf16[4,64,384]{2,1,0:T(8,128)(2,1)S(1)} %gather_heads.1.refs_4_), channel_id=1, source_target_pairs={{0,2},{1,3},{2,0},{3,1},{4,6},{5,7},{6,4},{7,5},{8,10},{9,11},{10,... | collective-permute-start | bytes 589832 | tf_op jit(solution)/shard_map/ppermute | solution.py:41
  67.3 5.8 %collective-permute-done.13.refs_6_ = bf16[4,64,384]{2,1,0:T(8,128)(2,1)S(1)} collective-permute-done((bf16[4,64,384]{2,1,0:T(8,128)(2,1)S(1)}, bf16[4,64,384]{2,1,0:T(8,128)(2,1)S(1)}, u32[]{:S(2)}, u32[]{:S(2)}) %collective-permute-start.13) | collective-permute-done | bytes 196640 | tf_op jit(solution)/shard_map/ppermute | solution.py:41
  73.0 1.4 %collective-permute-done.14.refs_7_ = bf16[4,64,384]{2,1,0:T(8,128)(2,1)S(1)} collective-permute-done((bf16[4,64,384]{2,1,0:T(8,128)(2,1)S(1)}, bf16[4,64,384]{2,1,0:T(8,128)(2,1)S(1)}, u32[]{:S(2)}, u32[]{:S(2)}) %collective-permute-start.14) | collective-permute-done | bytes 196640 | tf_op jit(solution)/shard_map/ppermute | solution.py:41
  74.5 3.5 %feed.1 = (bf16[384,256]{1,0:T(8,128)(2,1)S(1)}, bf16[384,256]{1,0:T(8,128)(2,1)S(1)}, bf16[384,256]{1,0:T(8,128)(2,1)S(1)}, bf16[384,256]{1,0:T(8,128)(2,1)S(1)}, f32[384,256]{1,0:T(8,128)S(1)}) custom-call(s32[3]{0:T(128)S(1)} %pad_add_fusion.place, bf16[384,256]{1,0:T(8,128)(2,1)S(1)} %get-tuple-element.32.own.refs_0_, ...), custom_call_target="tpu_custom_call" | custom-call | tf_op jit(solution)/shard_map/feed/pallas_call | solution.py:322
  78.6 0.9 %collective-permute-done.18 = bf16[384,256]{1,0:T(8,128)(2,1)S(1)} collective-permute-done((bf16[384,256]{1,0:T(8,128)(2,1)S(1)}, bf16[384,256]{1,0:T(8,128)(2,1)S(1)}, u32[]{:S(2)}, u32[]{:S(2)}) %collective-permute-start.18) | collective-permute-done | bytes 196640 | tf_op jit(solution)/shard_map/ppermute | solution.py:41
  79.6 1.2 %collective-permute-start.19 = (bf16[384,256]{1,0:T(8,128)(2,1)S(1)}, bf16[384,256]{1,0:T(8,128)(2,1)S(1)}, u32[]{:S(2)}, u32[]{:S(2)}) collective-permute-start(bf16[384,256]{1,0:T(8,128)(2,1)S(1)} %add_convert_fusion.1), channel_id=1, source_target_pairs={{0,2},{1,3},{2,0},{3,1},{4,6},{5,7},{6,4},{7,5},{8,10},{9,11},{10,... | collective-permute-start | bytes 589832 | tf_op jit(solution)/shard_map/ppermute | solution.py:41
  80.8 5.8 %collective-permute-done.19 = bf16[384,256]{1,0:T(8,128)(2,1)S(1)} collective-permute-done((bf16[384,256]{1,0:T(8,128)(2,1)S(1)}, bf16[384,256]{1,0:T(8,128)(2,1)S(1)}, u32[]{:S(2)}, u32[]{:S(2)}) %collective-permute-start.19) | collective-permute-done | bytes 196640 | tf_op jit(solution)/shard_map/ppermute | solution.py:41
  86.6 0.8 add_convert_fusion
  (34 shorter events, 2.8 us)
Async XLA Ops:
  0.0 6.9 %collective-permute-start.1 = (bf16[384,256]{1,0:T(8,128)(2,1)}, bf16[384,256]{1,0:T(8,128)(2,1)S(1)}, u32[]{:S(2)}, u32[]{:S(2)}) collective-permute-start(bf16[384,256]{1,0:T(8,128)(2,1)} %own.1), channel_id=1, source_target_pairs={{0,2},{1,3},{2,0},{3,1},{4,6},{5,7},{6,4},{7,5},{8,10},{9,11},{10,... | collective-permute-start | bytes 589832 | tf_op jit(solution)/shard_map/ppermute | solution.py:41
  1.2 9.8 %collective-permute-start = (bf16[384,256]{1,0:T(8,128)(2,1)}, bf16[384,256]{1,0:T(8,128)(2,1)S(1)}, u32[]{:S(2)}, u32[]{:S(2)}) collective-permute-start(bf16[384,256]{1,0:T(8,128)(2,1)} %own.1), channel_id=1, source_target_pairs={{0,1},{1,0},{2,3},{3,2},{4,5},{5,4},{6,7},{7,6},{8,9},{9,8},{10,11... | collective-permute-start | bytes 589832 | tf_op jit(solution)/shard_map/ppermute | solution.py:41
  6.9 4.2 %collective-permute-start.2 = (bf16[384,256]{1,0:T(8,128)(2,1)S(1)}, bf16[384,256]{1,0:T(8,128)(2,1)S(1)}, u32[]{:S(2)}, u32[]{:S(2)}) collective-permute-start(bf16[384,256]{1,0:T(8,128)(2,1)S(1)} %collective-permute-done.1.far.refs_2_), channel_id=1, source_target_pairs={{0,1},{1,0},{2,3},{3,2},{4,5},{5,4},{6,7},{7,6},{8,9},{9,8},{10,11... | collective-permute-start | bytes 589832 | tf_op jit(solution)/shard_map/ppermute | solution.py:41
  7.5 1.4 %copy-start.2 = (bf16[3,1024,256]{2,1,0:T(8,128)(2,1)S(1)}, bf16[3,1024,256]{2,1,0:T(8,128)(2,1)}, u32[]{:S(2)}) copy-start(bf16[3,1024,256]{2,1,0:T(8,128)(2,1)} %weights.1) | copy-start | bytes 4718596
  8.9 0.9 %copy-start.4 = (bf16[384,256]{1,0:T(8,128)(2,1)S(1)}, bf16[384,256]{1,0:T(8,128)(2,1)}, u32[]{:S(2)}) copy-start(bf16[384,256]{1,0:T(8,128)(2,1)} %own.1) | copy-start | bytes 589828
  9.9 0.7 copy-start.6
  10.6 8.1 %copy-start.3 = (bf16[256,1024]{1,0:T(8,128)(2,1)S(1)}, bf16[256,1024]{1,0:T(8,128)(2,1)}, u32[]{:S(2)}) copy-start(bf16[256,1024]{1,0:T(8,128)(2,1)} %refs_8_) | copy-start | bytes 1572868
  12.8 7.7 %collective-permute-start.3 = (bf16[200,384]{1,0:T(8,128)(2,1)S(1)}, bf16[200,384]{1,0:T(8,128)(2,1)S(1)}, u32[]{:S(2)}, u32[]{:S(2)}) collective-permute-start(bf16[200,384]{1,0:T(8,128)(2,1)S(1)} %get-tuple-element.37), channel_id=1, source_target_pairs={{0,4},{1,5},{2,6},{3,7},{4,8},{5,9},{6,10},{7,11},{8,12},{9,13},{1... | collective-permute-start | bytes 460808 | tf_op jit(solution)/shard_map/ppermute | solution.py:41
  14.4 10.6 %collective-permute-start.4 = (bf16[200,384]{1,0:T(8,128)(2,1)S(1)}, bf16[200,384]{1,0:T(8,128)(2,1)S(1)}, u32[]{:S(2)}, u32[]{:S(2)}) collective-permute-start(bf16[200,384]{1,0:T(8,128)(2,1)S(1)} %get-tuple-element.38), channel_id=1, source_target_pairs={{0,8},{1,9},{2,10},{3,11},{4,12},{5,13},{6,14},{7,15},{8,0},{9,1},... | collective-permute-start | bytes 460808 | tf_op jit(solution)/shard_map/ppermute | solution.py:41
  17.3 7.7 %collective-permute-start.5 = (bf16[200,384]{1,0:T(8,128)(2,1)S(1)}, bf16[200,384]{1,0:T(8,128)(2,1)S(1)}, u32[]{:S(2)}, u32[]{:S(2)}) collective-permute-start(bf16[200,384]{1,0:T(8,128)(2,1)S(1)} %get-tuple-element.39), channel_id=1, source_target_pairs={{0,12},{1,13},{2,14},{3,15},{4,0},{5,1},{6,2},{7,3},{8,4},{9,5},{1... | collective-permute-start | bytes 460808 | tf_op jit(solution)/shard_map/ppermute | solution.py:41
  18.7 46.8 %collective-permute-start.11 = (bf16[256,1024]{1,0:T(8,128)(2,1)S(1)}, bf16[256,1024]{1,0:T(8,128)(2,1)S(1)}, u32[]{:S(2)}, u32[]{:S(2)}) collective-permute-start(bf16[256,1024]{1,0:T(8,128)(2,1)S(1)} %copy-done.3), channel_id=1, source_target_pairs={{0,2},{1,3},{2,0},{3,1},{4,6},{5,7},{6,4},{7,5},{8,10},{9,11},{10,... | collective-permute-start | bytes 1572872 | tf_op jit(solution)/shard_map/ppermute | solution.py:41
  25.1 25.0 %collective-permute-start.7 = (bf16[4,136,384]{2,1,0:T(8,128)(2,1)S(1)}, bf16[4,136,384]{2,1,0:T(8,128)(2,1)S(1)}, u32[]{:S(2)}, u32[]{:S(2)}) collective-permute-start(bf16[4,136,384]{2,1,0:T(8,128)(2,1)S(1)} %get-tuple-element.41.refs_1_.refs_2_), channel_id=1, source_target_pairs={{0,16},{1,17},{2,18},{3,19},{4,20},{5,21},{6,22},{7,23},{8,24},{9,... | collective-permute-start | bytes 1253384 | tf_op jit(solution)/shard_map/ppermute | solution.py:41
  27.9 26.2 %collective-permute-start.6 = (bf16[4,136,384]{2,1,0:T(8,128)(2,1)S(1)}, bf16[4,136,384]{2,1,0:T(8,128)(2,1)S(1)}, u32[]{:S(2)}, u32[]{:S(2)}) collective-permute-start(bf16[4,136,384]{2,1,0:T(8,128)(2,1)S(1)} %get-tuple-element.41.refs_1_.refs_2_), channel_id=1, source_target_pairs={{16,0},{17,1},{18,2},{19,3},{20,4},{21,5},{22,6},{23,7},{24,8},{25... | collective-permute-start | bytes 1253384 | tf_op jit(solution)/shard_map/ppermute | solution.py:41
  32.4 42.1 %copy-start = (bf16[1024,1024]{1,0:T(8,128)(2,1)S(1)}, bf16[1024,1024]{1,0:T(8,128)(2,1)}, u32[]{:S(2)}) copy-start(bf16[1024,1024]{1,0:T(8,128)(2,1)} %refs_13_.1) | copy-start | bytes 6291460
  32.4 42.1 %copy-start.1 = (bf16[1024,1024]{1,0:T(8,128)(2,1)S(1)}, bf16[1024,1024]{1,0:T(8,128)(2,1)}, u32[]{:S(2)}) copy-start(bf16[1024,1024]{1,0:T(8,128)(2,1)} %refs_14_.1) | copy-start | bytes 6291460
  32.4 42.1 %copy-start.5 = (f32[1024]{0:T(1024)S(1)}, f32[1024]{0:T(1024)}, u32[]{:S(2)}) copy-start(f32[1024]{0:T(1024)} %param.13) | copy-start | bytes 12292
  58.2 5.4 %collective-permute-start.8 = (bf16[64,384]{1,0:T(8,128)(2,1)S(1)}, bf16[64,384]{1,0:T(8,128)(2,1)S(1)}, u32[]{:S(2)}, u32[]{:S(2)}) collective-permute-start(bf16[64,384]{1,0:T(8,128)(2,1)S(1)} %get-tuple-element.47), channel_id=1, source_target_pairs={{0,4},{1,5},{2,6},{3,7},{4,8},{5,9},{6,10},{7,11},{8,12},{9,13},{1... | collective-permute-start | bytes 147464 | tf_op jit(solution)/shard_map/ppermute | solution.py:41
  58.9 5.6 %collective-permute-start.9 = (bf16[64,384]{1,0:T(8,128)(2,1)S(1)}, bf16[64,384]{1,0:T(8,128)(2,1)S(1)}, u32[]{:S(2)}, u32[]{:S(2)}) collective-permute-start(bf16[64,384]{1,0:T(8,128)(2,1)S(1)} %get-tuple-element.48), channel_id=1, source_target_pairs={{0,8},{1,9},{2,10},{3,11},{4,12},{5,13},{6,14},{7,15},{8,0},{9,1},... | collective-permute-start | bytes 147464 | tf_op jit(solution)/shard_map/ppermute | solution.py:41
  60.8 4.1 %collective-permute-start.10 = (bf16[64,384]{1,0:T(8,128)(2,1)S(1)}, bf16[64,384]{1,0:T(8,128)(2,1)S(1)}, u32[]{:S(2)}, u32[]{:S(2)}) collective-permute-start(bf16[64,384]{1,0:T(8,128)(2,1)S(1)} %get-tuple-element.49), channel_id=1, source_target_pairs={{0,12},{1,13},{2,14},{3,15},{4,0},{5,1},{6,2},{7,3},{8,4},{9,5},{1... | collective-permute-start | bytes 147464 | tf_op jit(solution)/shard_map/ppermute | solution.py:41
  65.5 9.0 %collective-permute-start.15 = (bf16[256,1024]{1,0:T(8,128)(2,1)S(1)}, bf16[256,1024]{1,0:T(8,128)(2,1)S(1)}, u32[]{:S(2)}, u32[]{:S(2)}) collective-permute-start(bf16[256,1024]{1,0:T(8,128)(2,1)S(1)} %copy-done.3), channel_id=1, source_target_pairs={{0,1},{1,0},{2,3},{3,2},{4,5},{5,4},{6,7},{7,6},{8,9},{9,8},{10,11... | collective-permute-start | bytes 1572872 | tf_op jit(solution)/shard_map/ppermute | solution.py:41
  65.6 8.9 %collective-permute-start.16 = (bf16[256,1024]{1,0:T(8,128)(2,1)S(1)}, bf16[256,1024]{1,0:T(8,128)(2,1)S(1)}, u32[]{:S(2)}, u32[]{:S(2)}) collective-permute-start(bf16[256,1024]{1,0:T(8,128)(2,1)S(1)} %collective-permute-done.11.refs_10_), channel_id=1, source_target_pairs={{0,1},{1,0},{2,3},{3,2},{4,5},{5,4},{6,7},{7,6},{8,9},{9,8},{10,11... | collective-permute-start | bytes 1572872 | tf_op jit(solution)/shard_map/ppermute | solution.py:41
  66.1 6.9 %collective-permute-start.13 = (bf16[4,64,384]{2,1,0:T(8,128)(2,1)S(1)}, bf16[4,64,384]{2,1,0:T(8,128)(2,1)S(1)}, u32[]{:S(2)}, u32[]{:S(2)}) collective-permute-start(bf16[4,64,384]{2,1,0:T(8,128)(2,1)S(1)} %gather_heads.1.refs_4_), channel_id=1, source_target_pairs={{0,2},{1,3},{2,0},{3,1},{4,6},{5,7},{6,4},{7,5},{8,10},{9,11},{10,... | collective-permute-start | bytes 589832 | tf_op jit(solution)/shard_map/ppermute | solution.py:41
  67.3 5.8 %collective-permute-start.12 = (bf16[4,64,384]{2,1,0:T(8,128)(2,1)S(1)}, bf16[4,64,384]{2,1,0:T(8,128)(2,1)S(1)}, u32[]{:S(2)}, u32[]{:S(2)}) collective-permute-start(bf16[4,64,384]{2,1,0:T(8,128)(2,1)S(1)} %gather_heads.1.refs_4_), channel_id=1, source_target_pairs={{0,1},{1,0},{2,3},{3,2},{4,5},{5,4},{6,7},{7,6},{8,9},{9,8},{10,11... | collective-permute-start | bytes 589832 | tf_op jit(solution)/shard_map/ppermute | solution.py:41
  73.0 1.4 %collective-permute-start.14 = (bf16[4,64,384]{2,1,0:T(8,128)(2,1)S(1)}, bf16[4,64,384]{2,1,0:T(8,128)(2,1)S(1)}, u32[]{:S(2)}, u32[]{:S(2)}) collective-permute-start(bf16[4,64,384]{2,1,0:T(8,128)(2,1)S(1)} %collective-permute-done.13.refs_6_), channel_id=1, source_target_pairs={{0,1},{1,0},{2,3},{3,2},{4,5},{5,4},{6,7},{7,6},{8,9},{9,8},{10,11... | collective-permute-start | bytes 589832 | tf_op jit(solution)/shard_map/ppermute | solution.py:41
  78.0 1.5 %collective-permute-start.18 = (bf16[384,256]{1,0:T(8,128)(2,1)S(1)}, bf16[384,256]{1,0:T(8,128)(2,1)S(1)}, u32[]{:S(2)}, u32[]{:S(2)}) collective-permute-start(bf16[384,256]{1,0:T(8,128)(2,1)S(1)} %get-tuple-element.58), channel_id=1, source_target_pairs={{0,1},{1,0},{2,3},{3,2},{4,5},{5,4},{6,7},{7,6},{8,9},{9,8},{10,11... | collective-permute-start | bytes 589832 | tf_op jit(solution)/shard_map/ppermute | solution.py:41
  78.2 2.6 %collective-permute-start.17 = (bf16[384,256]{1,0:T(8,128)(2,1)S(1)}, bf16[384,256]{1,0:T(8,128)(2,1)S(1)}, u32[]{:S(2)}, u32[]{:S(2)}) collective-permute-start(bf16[384,256]{1,0:T(8,128)(2,1)S(1)} %get-tuple-element.56), channel_id=1, source_target_pairs={{0,1},{1,0},{2,3},{3,2},{4,5},{5,4},{6,7},{7,6},{8,9},{9,8},{10,11... | collective-permute-start | bytes 589832 | tf_op jit(solution)/shard_map/ppermute | solution.py:41
  79.6 7.0 %collective-permute-start.19 = (bf16[384,256]{1,0:T(8,128)(2,1)S(1)}, bf16[384,256]{1,0:T(8,128)(2,1)S(1)}, u32[]{:S(2)}, u32[]{:S(2)}) collective-permute-start(bf16[384,256]{1,0:T(8,128)(2,1)S(1)} %add_convert_fusion.1), channel_id=1, source_target_pairs={{0,2},{1,3},{2,0},{3,1},{4,6},{5,7},{6,4},{7,5},{8,10},{9,11},{10,... | collective-permute-start | bytes 589832 | tf_op jit(solution)/shard_map/ppermute | solution.py:41

commit v3 on v1

--- a/solution.py
+++ b/solution.py
@@ -350,18 +350,21 @@
     w_late, _ = lax.optimization_barrier((w_out, parts[2]))
     w_far = send(w_late, to_chip)
     sides = pack(arrived)
-    lower, upper = send(sides, to_super(1)), send(sides, to_super(-1))
+    lower = send(sides, to_super(1))
+    upper = send(sides, to_super(-1))
     late = lax.optimization_barrier((*made[1:4], sides))
-    queries = [made[0]] + [send(late[d - 1], to_y(d)) for d in range(1, 4)]
+    queries = [made[0]]
+    for d in range(1, 4):
+        queries.append(send(late[d - 1], to_y(d)))
     state = attend(queries, sides, sides, None, False)
-    w_own, w_far, *state = lax.optimization_barrier((w_late, w_far, *state))
-    outers = [w_own, send(w_own, to_core), w_far, send(w_far, to_core)]
     state = attend(queries, sides, lower, state, False)
     mixed = attend(queries, sides, upper, state, True)
     chunks = [mixed[0]] + [None] * 3
     for d in range(1, 4):
         chunks[(4 - d) % 4] = send(mixed[d], to_y(-d))
-    heads = everyone(gather_heads(place, chunks))
+    gathered, w_own, w_far = lax.optimization_barrier((gather_heads(place, chunks), w_late, w_far))
+    heads = everyone(gathered)
+    outers = [w_own, send(w_own, to_core), w_far, send(w_far, to_core)]
     far_keep, far_give, near_keep, near_give, share = feed(
         place, parts, heads, outers, norm2_gain[None, :], w_up, w_down
     )

time: 87.1 us -> 87.8 us (level)
  the two profiles are of different devices: /device:TPU:128 before, /device:TPU:132 now
where the time goes in v3:
time: 87.8 us; the launch traced here: 87.6 us
  waiting for transfers between devices  33.8 us (38%)
  starting transfers between devices  27.4 us (31%)
  Pallas kernels  21.6 us (25%)
  local copies, waits for them, and re-layouts  3.72 us (4%)
  other arithmetic  0.91 us (1%)
    ppermute x23, waiting for transfers between devices, send(): return lax.ppermute(block, AXES, route)  33.8 us
    ppermute x23, starting transfers between devices, send(): return lax.ppermute(block, AXES, route)  27.4 us
    pallas_call x3, Pallas kernels, attend(): pl.pallas_call(body, out_shape=out, in_specs=[VMEM] * len(args), out_spec...  15.4 us
    pallas_call x1, Pallas kernels, feed(): pl.pallas_call(feed_body, name='feed', out_shape=[jax.ShapeDtypeStruct((r...  3.46 us
    unnamed x14, local copies, waits for them, and re-layouts  3.03 us
  transfers between devices with their start and end apart: 23, of which 13 were waited for; matrix products, arithmetic and copies ran while one was open for 1% of the time, Pallas kernels for 19%

profile of v3, /device:TPU:132, one launch (start us, length us, event | category | flops | bytes accessed | tf_op | source)
XLA Modules:
  0.0 87.6 jit_solution(9121082387881838246)
XLA Ops:
  0.0 1.2 %collective-permute-start.1 = (bf16[384,256]{1,0:T(8,128)(2,1)}, bf16[384,256]{1,0:T(8,128)(2,1)S(1)}, u32[]{:S(2)}, u32[]{:S(2)}) collective-permute-start(bf16[384,256]{1,0:T(8,128)(2,1)} %own.1), channel_id=1, source_target_pairs={{0,2},{1,3},{2,0},{3,1},{4,6},{5,7},{6,4},{7,5},{8,10},{9,11},{10,... | collective-permute-start | bytes 589832 | tf_op jit(solution)/shard_map/ppermute | solution.py:41
  1.2 5.7 %collective-permute-done.1.far.refs_2_ = bf16[384,256]{1,0:T(8,128)(2,1)S(1)} collective-permute-done((bf16[384,256]{1,0:T(8,128)(2,1)}, bf16[384,256]{1,0:T(8,128)(2,1)S(1)}, u32[]{:S(2)}, u32[]{:S(2)}) %collective-permute-start.1) | collective-permute-done | bytes 196640 | tf_op jit(solution)/shard_map/ppermute | solution.py:41
  7.5 1.4 %copy-done.2 = bf16[3,1024,256]{2,1,0:T(8,128)(2,1)S(1)} copy-done((bf16[3,1024,256]{2,1,0:T(8,128)(2,1)S(1)}, bf16[3,1024,256]{2,1,0:T(8,128)(2,1)}, u32[]{:S(2)}) %copy-start.2) | copy-done | bytes 1572888
  9.0 0.9 %copy-done.4 = bf16[384,256]{1,0:T(8,128)(2,1)S(1)} copy-done((bf16[384,256]{1,0:T(8,128)(2,1)S(1)}, bf16[384,256]{1,0:T(8,128)(2,1)}, u32[]{:S(2)}) %copy-start.4) | copy-done | bytes 196632
  11.0 1.7 %project.1 = (bf16[64,384]{1,0:T(8,128)(2,1)S(1)}, bf16[64,384]{1,0:T(8,128)(2,1)S(1)}, bf16[64,384]{1,0:T(8,128)(2,1)S(1)}, bf16[64,384]{1,0:T(8,128)(2,1)S(1)}...) custom-call(s32[3]{0:T(128)S(1)} %pad_add_fusion.place, ...), custom_call_target="tpu_custom_call" | custom-call | tf_op jit(solution)/shard_map/project/pallas_call | solution.py:137
  12.8 1.7 %collective-permute-start.3 = (bf16[136,384]{1,0:T(8,128)(2,1)S(1)}, bf16[136,384]{1,0:T(8,128)(2,1)S(1)}, u32[]{:S(2)}, u32[]{:S(2)}) collective-permute-start(bf16[136,384]{1,0:T(8,128)(2,1)S(1)} %get-tuple-element.46), channel_id=1, source_target_pairs={{0,4},{1,5},{2,6},{3,7},{4,8},{5,9},{6,10},{7,11},{8,12},{9,13},{1... | collective-permute-start | bytes 313352 | tf_op jit(solution)/shard_map/ppermute | solution.py:41
  14.4 2.9 %collective-permute-start.4 = (bf16[136,384]{1,0:T(8,128)(2,1)S(1)}, bf16[136,384]{1,0:T(8,128)(2,1)S(1)}, u32[]{:S(2)}, u32[]{:S(2)}) collective-permute-start(bf16[136,384]{1,0:T(8,128)(2,1)S(1)} %get-tuple-element.47), channel_id=1, source_target_pairs={{0,8},{1,9},{2,10},{3,11},{4,12},{5,13},{6,14},{7,15},{8,0},{9,1},... | collective-permute-start | bytes 313352 | tf_op jit(solution)/shard_map/ppermute | solution.py:41
  17.3 1.3 %collective-permute-start.5 = (bf16[136,384]{1,0:T(8,128)(2,1)S(1)}, bf16[136,384]{1,0:T(8,128)(2,1)S(1)}, u32[]{:S(2)}, u32[]{:S(2)}) collective-permute-start(bf16[136,384]{1,0:T(8,128)(2,1)S(1)} %get-tuple-element.48), channel_id=1, source_target_pairs={{0,12},{1,13},{2,14},{3,15},{4,0},{5,1},{6,2},{7,3},{8,4},{9,5},{1... | collective-permute-start | bytes 313352 | tf_op jit(solution)/shard_map/ppermute | solution.py:41
  18.7 1.2 %collective-permute-start.14 = (bf16[256,1024]{1,0:T(8,128)(2,1)S(1)}, bf16[256,1024]{1,0:T(8,128)(2,1)S(1)}, u32[]{:S(2)}, u32[]{:S(2)}) collective-permute-start(bf16[256,1024]{1,0:T(8,128)(2,1)S(1)} %copy-done.3), channel_id=1, source_target_pairs={{0,2},{1,3},{2,0},{3,1},{4,6},{5,7},{6,4},{7,5},{8,10},{9,11},{10,... | collective-permute-start | bytes 1572872 | tf_op jit(solution)/shard_map/ppermute | solution.py:41
  19.9 3.0 %collective-permute-done.4.third = bf16[136,384]{1,0:T(8,128)(2,1)S(1)} collective-permute-done((bf16[136,384]{1,0:T(8,128)(2,1)S(1)}, bf16[136,384]{1,0:T(8,128)(2,1)S(1)}, u32[]{:S(2)}, u32[]{:S(2)}) %collective-permute-start.4) | collective-permute-done | bytes 104480 | tf_op jit(solution)/shard_map/ppermute | solution.py:41
  22.9 2.9 %collective-permute-start.10 = (bf16[4,136,384]{2,1,0:T(8,128)(2,1)S(1)}, bf16[4,136,384]{2,1,0:T(8,128)(2,1)S(1)}, u32[]{:S(2)}, u32[]{:S(2)}) collective-permute-start(bf16[4,136,384]{2,1,0:T(8,128)(2,1)S(1)} %pack.1.refs_4_.refs_5_), channel_id=1, source_target_pairs={{0,16},{1,17},{2,18},{3,19},{4,20},{5,21},{6,22},{7,23},{8,24},{9,... | collective-permute-start | bytes 1253384 | tf_op jit(solution)/shard_map/ppermute | solution.py:41
  25.8 4.5 %collective-permute-start.9 = (bf16[4,136,384]{2,1,0:T(8,128)(2,1)S(1)}, bf16[4,136,384]{2,1,0:T(8,128)(2,1)S(1)}, u32[]{:S(2)}, u32[]{:S(2)}) collective-permute-start(bf16[4,136,384]{2,1,0:T(8,128)(2,1)S(1)} %pack.1.refs_4_.refs_5_), channel_id=1, source_target_pairs={{16,0},{17,1},{18,2},{19,3},{20,4},{21,5},{22,6},{23,7},{24,8},{25... | collective-permute-start | bytes 1253384 | tf_op jit(solution)/shard_map/ppermute | solution.py:41
  30.3 1.3 %collective-permute-start.6 = (bf16[64,384]{1,0:T(8,128)(2,1)S(1)}, bf16[64,384]{1,0:T(8,128)(2,1)S(1)}, u32[]{:S(2)}, u32[]{:S(2)}) collective-permute-start(bf16[64,384]{1,0:T(8,128)(2,1)S(1)} %get-tuple-element.49), channel_id=1, source_target_pairs={{0,4},{1,5},{2,6},{3,7},{4,8},{5,9},{6,10},{7,11},{8,12},{9,13},{1... | collective-permute-start | bytes 147464 | tf_op jit(solution)/shard_map/ppermute | solution.py:41
  31.6 2.4 %collective-permute-start.7 = (bf16[64,384]{1,0:T(8,128)(2,1)S(1)}, bf16[64,384]{1,0:T(8,128)(2,1)S(1)}, u32[]{:S(2)}, u32[]{:S(2)}) collective-permute-start(bf16[64,384]{1,0:T(8,128)(2,1)S(1)} %get-tuple-element.50), channel_id=1, source_target_pairs={{0,8},{1,9},{2,10},{3,11},{4,12},{5,13},{6,14},{7,15},{8,0},{9,1},... | collective-permute-start | bytes 147464 | tf_op jit(solution)/shard_map/ppermute | solution.py:41
  34.0 1.7 %collective-permute-done.6.refs_1_ = bf16[64,384]{1,0:T(8,128)(2,1)S(1)} collective-permute-done((bf16[64,384]{1,0:T(8,128)(2,1)S(1)}, bf16[64,384]{1,0:T(8,128)(2,1)S(1)}, u32[]{:S(2)}, u32[]{:S(2)}) %collective-permute-start.6) | collective-permute-done | bytes 49184 | tf_op jit(solution)/shard_map/ppermute | solution.py:41
  35.7 1.0 %collective-permute-start.8 = (bf16[64,384]{1,0:T(8,128)(2,1)S(1)}, bf16[64,384]{1,0:T(8,128)(2,1)S(1)}, u32[]{:S(2)}, u32[]{:S(2)}) collective-permute-start(bf16[64,384]{1,0:T(8,128)(2,1)S(1)} %get-tuple-element.51), channel_id=1, source_target_pairs={{0,12},{1,13},{2,14},{3,15},{4,0},{5,1},{6,2},{7,3},{8,4},{9,5},{1... | collective-permute-start | bytes 147464 | tf_op jit(solution)/shard_map/ppermute | solution.py:41
  37.2 2.6 %collective-permute-done.8.refs_3_ = bf16[64,384]{1,0:T(8,128)(2,1)S(1)} collective-permute-done((bf16[64,384]{1,0:T(8,128)(2,1)S(1)}, bf16[64,384]{1,0:T(8,128)(2,1)S(1)}, u32[]{:S(2)}, u32[]{:S(2)}) %collective-permute-start.8) | collective-permute-done | bytes 49184 | tf_op jit(solution)/shard_map/ppermute | solution.py:41
  39.8 7.1 %shard_map.82 = (f32[4,1,384]{2,1,0:T(1,128)S(1)}, f32[4,80,384]{2,1,0:T(8,128)S(1)}) custom-call(bf16[64,384]{1,0:T(8,128)(2,1)S(1)} %get-tuple-element.41.refs_0_, bf16[64,384]{1,0:T(8,128)(2,1)S(1)} %collective-permute-done.6.refs_1_, bf16[64,384]{1,0:T(8,128)(2,1)S(1)} %collective-permute-done.7.refs_2_, ...), custom_call_target="tpu_custom_call" | custom-call | tf_op jit(solution)/shard_map/pallas_call | solution.py:255
  46.9 3.2 %collective-permute-done.10.refs_5_ = bf16[4,136,384]{2,1,0:T(8,128)(2,1)S(1)} collective-permute-done((bf16[4,136,384]{2,1,0:T(8,128)(2,1)S(1)}, bf16[4,136,384]{2,1,0:T(8,128)(2,1)S(1)}, u32[]{:S(2)}, u32[]{:S(2)}) %collective-permute-start.10) | collective-permute-done | bytes 417824 | tf_op jit(solution)/shard_map/ppermute | solution.py:41
  50.1 4.1 %shard_map.83 = (f32[4,1,384]{2,1,0:T(1,128)S(1)}, f32[4,80,384]{2,1,0:T(8,128)S(1)}) custom-call(bf16[64,384]{1,0:T(8,128)(2,1)S(1)} %get-tuple-element.41.refs_0_, bf16[64,384]{1,0:T(8,128)(2,1)S(1)} %collective-permute-done.6.refs_1_, bf16[64,384]{1,0:T(8,128)(2,1)S(1)} %collective-permute-done.7.refs_2_, ...), custom_call_target="tpu_custom_call" | custom-call | tf_op jit(solution)/shard_map/pallas_call | solution.py:255
  54.2 4.2 %shard_map.84 = (bf16[64,384]{1,0:T(8,128)(2,1)S(1)}, bf16[64,384]{1,0:T(8,128)(2,1)S(1)}, bf16[64,384]{1,0:T(8,128)(2,1)S(1)}, bf16[64,384]{1,0:T(8,128)(2,1)S(1)}) custom-call(bf16[64,384]{1,0:T(8,128)(2,1)S(1)} %get-tuple-element.41.refs_0_, bf16[64,384]{1,0:T(8,128)(2,1)S(1)} %collective-permute-done.6.refs_1_, ...), custom_call_target="tpu_custom_call" | custom-call | tf_op jit(solution)/shard_map/pallas_call | solution.py:255
  59.1 1.1 %collective-permute-start.12 = (bf16[64,384]{1,0:T(8,128)(2,1)S(1)}, bf16[64,384]{1,0:T(8,128)(2,1)S(1)}, u32[]{:S(2)}, u32[]{:S(2)}) collective-permute-start(bf16[64,384]{1,0:T(8,128)(2,1)S(1)} %get-tuple-element.58), channel_id=1, source_target_pairs={{0,8},{1,9},{2,10},{3,11},{4,12},{5,13},{6,14},{7,15},{8,0},{9,1},... | collective-permute-start | bytes 147464 | tf_op jit(solution)/shard_map/ppermute | solution.py:41
  60.2 1.7 %collective-permute-start.13 = (bf16[64,384]{1,0:T(8,128)(2,1)S(1)}, bf16[64,384]{1,0:T(8,128)(2,1)S(1)}, u32[]{:S(2)}, u32[]{:S(2)}) collective-permute-start(bf16[64,384]{1,0:T(8,128)(2,1)S(1)} %get-tuple-element.59), channel_id=1, source_target_pairs={{0,12},{1,13},{2,14},{3,15},{4,0},{5,1},{6,2},{7,3},{8,4},{9,5},{1... | collective-permute-start | bytes 147464 | tf_op jit(solution)/shard_map/ppermute | solution.py:41
  61.9 1.8 %collective-permute-done.11.second = bf16[64,384]{1,0:T(8,128)(2,1)S(1)} collective-permute-done((bf16[64,384]{1,0:T(8,128)(2,1)S(1)}, bf16[64,384]{1,0:T(8,128)(2,1)S(1)}, u32[]{:S(2)}, u32[]{:S(2)}) %collective-permute-start.11) | collective-permute-done | bytes 49184 | tf_op jit(solution)/shard_map/ppermute | solution.py:41
  63.7 1.0 %collective-permute-done.12.third = bf16[64,384]{1,0:T(8,128)(2,1)S(1)} collective-permute-done((bf16[64,384]{1,0:T(8,128)(2,1)S(1)}, bf16[64,384]{1,0:T(8,128)(2,1)S(1)}, u32[]{:S(2)}, u32[]{:S(2)}) %collective-permute-start.12) | collective-permute-done | bytes 49184 | tf_op jit(solution)/shard_map/ppermute | solution.py:41
  66.3 1.1 %collective-permute-start.16 = (bf16[4,64,384]{2,1,0:T(8,128)(2,1)S(1)}, bf16[4,64,384]{2,1,0:T(8,128)(2,1)S(1)}, u32[]{:S(2)}, u32[]{:S(2)}) collective-permute-start(bf16[4,64,384]{2,1,0:T(8,128)(2,1)S(1)} %gather_heads.1.refs_4_), channel_id=1, source_target_pairs={{0,2},{1,3},{2,0},{3,1},{4,6},{5,7},{6,4},{7,5},{8,10},{9,11},{10,... | collective-permute-start | bytes 589832 | tf_op jit(solution)/shard_map/ppermute | solution.py:41
  67.4 5.8 %collective-permute-done.16.refs_6_ = bf16[4,64,384]{2,1,0:T(8,128)(2,1)S(1)} collective-permute-done((bf16[4,64,384]{2,1,0:T(8,128)(2,1)S(1)}, bf16[4,64,384]{2,1,0:T(8,128)(2,1)S(1)}, u32[]{:S(2)}, u32[]{:S(2)}) %collective-permute-start.16) | collective-permute-done | bytes 196640 | tf_op jit(solution)/shard_map/ppermute | solution.py:41
  73.2 1.4 %collective-permute-done.17.refs_7_ = bf16[4,64,384]{2,1,0:T(8,128)(2,1)S(1)} collective-permute-done((bf16[4,64,384]{2,1,0:T(8,128)(2,1)S(1)}, bf16[4,64,384]{2,1,0:T(8,128)(2,1)S(1)}, u32[]{:S(2)}, u32[]{:S(2)}) %collective-permute-start.17) | collective-permute-done | bytes 196640 | tf_op jit(solution)/shard_map/ppermute | solution.py:41
  74.7 3.5 %feed.1 = (bf16[384,256]{1,0:T(8,128)(2,1)S(1)}, bf16[384,256]{1,0:T(8,128)(2,1)S(1)}, bf16[384,256]{1,0:T(8,128)(2,1)S(1)}, bf16[384,256]{1,0:T(8,128)(2,1)S(1)}, f32[384,256]{1,0:T(8,128)S(1)}) custom-call(s32[3]{0:T(128)S(1)} %pad_add_fusion.place, bf16[384,256]{1,0:T(8,128)(2,1)S(1)} %get-tuple-element.37.own.refs_0_, ...), custom_call_target="tpu_custom_call" | custom-call | tf_op jit(solution)/shard_map/feed/pallas_call | solution.py:320
  78.8 0.9 %collective-permute-done.21 = bf16[384,256]{1,0:T(8,128)(2,1)S(1)} collective-permute-done((bf16[384,256]{1,0:T(8,128)(2,1)S(1)}, bf16[384,256]{1,0:T(8,128)(2,1)S(1)}, u32[]{:S(2)}, u32[]{:S(2)}) %collective-permute-start.21) | collective-permute-done | bytes 196640 | tf_op jit(solution)/shard_map/ppermute | solution.py:41
  79.7 1.2 %collective-permute-start.22 = (bf16[384,256]{1,0:T(8,128)(2,1)S(1)}, bf16[384,256]{1,0:T(8,128)(2,1)S(1)}, u32[]{:S(2)}, u32[]{:S(2)}) collective-permute-start(bf16[384,256]{1,0:T(8,128)(2,1)S(1)} %add_convert_fusion.1), channel_id=1, source_target_pairs={{0,2},{1,3},{2,0},{3,1},{4,6},{5,7},{6,4},{7,5},{8,10},{9,11},{10,... | collective-permute-start | bytes 589832 | tf_op jit(solution)/shard_map/ppermute | solution.py:41
  81.0 5.8 %collective-permute-done.22 = bf16[384,256]{1,0:T(8,128)(2,1)S(1)} collective-permute-done((bf16[384,256]{1,0:T(8,128)(2,1)S(1)}, bf16[384,256]{1,0:T(8,128)(2,1)S(1)}, u32[]{:S(2)}, u32[]{:S(2)}) %collective-permute-start.22) | collective-permute-done | bytes 196640 | tf_op jit(solution)/shard_map/ppermute | solution.py:41
  (40 shorter events, 6.3 us)
Async XLA Ops:
  0.0 6.9 %collective-permute-start.1 = (bf16[384,256]{1,0:T(8,128)(2,1)}, bf16[384,256]{1,0:T(8,128)(2,1)S(1)}, u32[]{:S(2)}, u32[]{:S(2)}) collective-permute-start(bf16[384,256]{1,0:T(8,128)(2,1)} %own.1), channel_id=1, source_target_pairs={{0,2},{1,3},{2,0},{3,1},{4,6},{5,7},{6,4},{7,5},{8,10},{9,11},{10,... | collective-permute-start | bytes 589832 | tf_op jit(solution)/shard_map/ppermute | solution.py:41
  1.2 9.8 %collective-permute-start = (bf16[384,256]{1,0:T(8,128)(2,1)}, bf16[384,256]{1,0:T(8,128)(2,1)S(1)}, u32[]{:S(2)}, u32[]{:S(2)}) collective-permute-start(bf16[384,256]{1,0:T(8,128)(2,1)} %own.1), channel_id=1, source_target_pairs={{0,1},{1,0},{2,3},{3,2},{4,5},{5,4},{6,7},{7,6},{8,9},{9,8},{10,11... | collective-permute-start | bytes 589832 | tf_op jit(solution)/shard_map/ppermute | solution.py:41
  6.9 4.2 %collective-permute-start.2 = (bf16[384,256]{1,0:T(8,128)(2,1)S(1)}, bf16[384,256]{1,0:T(8,128)(2,1)S(1)}, u32[]{:S(2)}, u32[]{:S(2)}) collective-permute-start(bf16[384,256]{1,0:T(8,128)(2,1)S(1)} %collective-permute-done.1.far.refs_2_), channel_id=1, source_target_pairs={{0,1},{1,0},{2,3},{3,2},{4,5},{5,4},{6,7},{7,6},{8,9},{9,8},{10,11... | collective-permute-start | bytes 589832 | tf_op jit(solution)/shard_map/ppermute | solution.py:41
  7.5 1.4 %copy-start.2 = (bf16[3,1024,256]{2,1,0:T(8,128)(2,1)S(1)}, bf16[3,1024,256]{2,1,0:T(8,128)(2,1)}, u32[]{:S(2)}) copy-start(bf16[3,1024,256]{2,1,0:T(8,128)(2,1)} %weights.1) | copy-start | bytes 4718596
  8.9 0.9 %copy-start.4 = (bf16[384,256]{1,0:T(8,128)(2,1)S(1)}, bf16[384,256]{1,0:T(8,128)(2,1)}, u32[]{:S(2)}) copy-start(bf16[384,256]{1,0:T(8,128)(2,1)} %own.1) | copy-start | bytes 589828
  9.9 0.7 copy-start.6
  10.6 8.1 %copy-start.3 = (bf16[256,1024]{1,0:T(8,128)(2,1)S(1)}, bf16[256,1024]{1,0:T(8,128)(2,1)}, u32[]{:S(2)}) copy-start(bf16[256,1024]{1,0:T(8,128)(2,1)} %refs_8_) | copy-start | bytes 1572868
  12.8 7.1 %collective-permute-start.3 = (bf16[136,384]{1,0:T(8,128)(2,1)S(1)}, bf16[136,384]{1,0:T(8,128)(2,1)S(1)}, u32[]{:S(2)}, u32[]{:S(2)}) collective-permute-start(bf16[136,384]{1,0:T(8,128)(2,1)S(1)} %get-tuple-element.46), channel_id=1, source_target_pairs={{0,4},{1,5},{2,6},{3,7},{4,8},{5,9},{6,10},{7,11},{8,12},{9,13},{1... | collective-permute-start | bytes 313352 | tf_op jit(solution)/shard_map/ppermute | solution.py:41
  14.4 8.5 %collective-permute-start.4 = (bf16[136,384]{1,0:T(8,128)(2,1)S(1)}, bf16[136,384]{1,0:T(8,128)(2,1)S(1)}, u32[]{:S(2)}, u32[]{:S(2)}) collective-permute-start(bf16[136,384]{1,0:T(8,128)(2,1)S(1)} %get-tuple-element.47), channel_id=1, source_target_pairs={{0,8},{1,9},{2,10},{3,11},{4,12},{5,13},{6,14},{7,15},{8,0},{9,1},... | collective-permute-start | bytes 313352 | tf_op jit(solution)/shard_map/ppermute | solution.py:41
  17.3 5.5 %collective-permute-start.5 = (bf16[136,384]{1,0:T(8,128)(2,1)S(1)}, bf16[136,384]{1,0:T(8,128)(2,1)S(1)}, u32[]{:S(2)}, u32[]{:S(2)}) collective-permute-start(bf16[136,384]{1,0:T(8,128)(2,1)S(1)} %get-tuple-element.48), channel_id=1, source_target_pairs={{0,12},{1,13},{2,14},{3,15},{4,0},{5,1},{6,2},{7,3},{8,4},{9,5},{1... | collective-permute-start | bytes 313352 | tf_op jit(solution)/shard_map/ppermute | solution.py:41
  18.7 47.0 %collective-permute-start.14 = (bf16[256,1024]{1,0:T(8,128)(2,1)S(1)}, bf16[256,1024]{1,0:T(8,128)(2,1)S(1)}, u32[]{:S(2)}, u32[]{:S(2)}) collective-permute-start(bf16[256,1024]{1,0:T(8,128)(2,1)S(1)} %copy-done.3), channel_id=1, source_target_pairs={{0,2},{1,3},{2,0},{3,1},{4,6},{5,7},{6,4},{7,5},{8,10},{9,11},{10,... | collective-permute-start | bytes 1572872 | tf_op jit(solution)/shard_map/ppermute | solution.py:41
  22.9 27.1 %collective-permute-start.10 = (bf16[4,136,384]{2,1,0:T(8,128)(2,1)S(1)}, bf16[4,136,384]{2,1,0:T(8,128)(2,1)S(1)}, u32[]{:S(2)}, u32[]{:S(2)}) collective-permute-start(bf16[4,136,384]{2,1,0:T(8,128)(2,1)S(1)} %pack.1.refs_4_.refs_5_), channel_id=1, source_target_pairs={{0,16},{1,17},{2,18},{3,19},{4,20},{5,21},{6,22},{7,23},{8,24},{9,... | collective-permute-start | bytes 1253384 | tf_op jit(solution)/shard_map/ppermute | solution.py:41
  25.8 28.3 %collective-permute-start.9 = (bf16[4,136,384]{2,1,0:T(8,128)(2,1)S(1)}, bf16[4,136,384]{2,1,0:T(8,128)(2,1)S(1)}, u32[]{:S(2)}, u32[]{:S(2)}) collective-permute-start(bf16[4,136,384]{2,1,0:T(8,128)(2,1)S(1)} %pack.1.refs_4_.refs_5_), channel_id=1, source_target_pairs={{16,0},{17,1},{18,2},{19,3},{20,4},{21,5},{22,6},{23,7},{24,8},{25... | collective-permute-start | bytes 1253384 | tf_op jit(solution)/shard_map/ppermute | solution.py:41
  30.3 5.4 %collective-permute-start.6 = (bf16[64,384]{1,0:T(8,128)(2,1)S(1)}, bf16[64,384]{1,0:T(8,128)(2,1)S(1)}, u32[]{:S(2)}, u32[]{:S(2)}) collective-permute-start(bf16[64,384]{1,0:T(8,128)(2,1)S(1)} %get-tuple-element.49), channel_id=1, source_target_pairs={{0,4},{1,5},{2,6},{3,7},{4,8},{5,9},{6,10},{7,11},{8,12},{9,13},{1... | collective-permute-start | bytes 147464 | tf_op jit(solution)/shard_map/ppermute | solution.py:41
  31.6 5.6 %collective-permute-start.7 = (bf16[64,384]{1,0:T(8,128)(2,1)S(1)}, bf16[64,384]{1,0:T(8,128)(2,1)S(1)}, u32[]{:S(2)}, u32[]{:S(2)}) collective-permute-start(bf16[64,384]{1,0:T(8,128)(2,1)S(1)} %get-tuple-element.50), channel_id=1, source_target_pairs={{0,8},{1,9},{2,10},{3,11},{4,12},{5,13},{6,14},{7,15},{8,0},{9,1},... | collective-permute-start | bytes 147464 | tf_op jit(solution)/shard_map/ppermute | solution.py:41
  35.7 4.1 %collective-permute-start.8 = (bf16[64,384]{1,0:T(8,128)(2,1)S(1)}, bf16[64,384]{1,0:T(8,128)(2,1)S(1)}, u32[]{:S(2)}, u32[]{:S(2)}) collective-permute-start(bf16[64,384]{1,0:T(8,128)(2,1)S(1)} %get-tuple-element.51), channel_id=1, source_target_pairs={{0,12},{1,13},{2,14},{3,15},{4,0},{5,1},{6,2},{7,3},{8,4},{9,5},{1... | collective-permute-start | bytes 147464 | tf_op jit(solution)/shard_map/ppermute | solution.py:41
  39.8 34.9 %copy-start = (bf16[1024,1024]{1,0:T(8,128)(2,1)S(1)}, bf16[1024,1024]{1,0:T(8,128)(2,1)}, u32[]{:S(2)}) copy-start(bf16[1024,1024]{1,0:T(8,128)(2,1)} %refs_13_.1) | copy-start | bytes 6291460
  39.8 34.9 %copy-start.1 = (bf16[1024,1024]{1,0:T(8,128)(2,1)S(1)}, bf16[1024,1024]{1,0:T(8,128)(2,1)}, u32[]{:S(2)}) copy-start(bf16[1024,1024]{1,0:T(8,128)(2,1)} %refs_14_.1) | copy-start | bytes 6291460
  39.8 34.9 %copy-start.5 = (f32[1024]{0:T(1024)S(1)}, f32[1024]{0:T(1024)}, u32[]{:S(2)}) copy-start(f32[1024]{0:T(1024)} %param.13) | copy-start | bytes 12292
  58.4 5.4 %collective-permute-start.11 = (bf16[64,384]{1,0:T(8,128)(2,1)S(1)}, bf16[64,384]{1,0:T(8,128)(2,1)S(1)}, u32[]{:S(2)}, u32[]{:S(2)}) collective-permute-start(bf16[64,384]{1,0:T(8,128)(2,1)S(1)} %get-tuple-element.57), channel_id=1, source_target_pairs={{0,4},{1,5},{2,6},{3,7},{4,8},{5,9},{6,10},{7,11},{8,12},{9,13},{1... | collective-permute-start | bytes 147464 | tf_op jit(solution)/shard_map/ppermute | solution.py:41
  59.1 5.6 %collective-permute-start.12 = (bf16[64,384]{1,0:T(8,128)(2,1)S(1)}, bf16[64,384]{1,0:T(8,128)(2,1)S(1)}, u32[]{:S(2)}, u32[]{:S(2)}) collective-permute-start(bf16[64,384]{1,0:T(8,128)(2,1)S(1)} %get-tuple-element.58), channel_id=1, source_target_pairs={{0,8},{1,9},{2,10},{3,11},{4,12},{5,13},{6,14},{7,15},{8,0},{9,1},... | collective-permute-start | bytes 147464 | tf_op jit(solution)/shard_map/ppermute | solution.py:41
  60.2 4.9 %collective-permute-start.13 = (bf16[64,384]{1,0:T(8,128)(2,1)S(1)}, bf16[64,384]{1,0:T(8,128)(2,1)S(1)}, u32[]{:S(2)}, u32[]{:S(2)}) collective-permute-start(bf16[64,384]{1,0:T(8,128)(2,1)S(1)} %get-tuple-element.59), channel_id=1, source_target_pairs={{0,12},{1,13},{2,14},{3,15},{4,0},{5,1},{6,2},{7,3},{8,4},{9,5},{1... | collective-permute-start | bytes 147464 | tf_op jit(solution)/shard_map/ppermute | solution.py:41
  65.7 9.0 %collective-permute-start.18 = (bf16[256,1024]{1,0:T(8,128)(2,1)S(1)}, bf16[256,1024]{1,0:T(8,128)(2,1)S(1)}, u32[]{:S(2)}, u32[]{:S(2)}) collective-permute-start(bf16[256,1024]{1,0:T(8,128)(2,1)S(1)} %copy-done.3), channel_id=1, source_target_pairs={{0,1},{1,0},{2,3},{3,2},{4,5},{5,4},{6,7},{7,6},{8,9},{9,8},{10,11... | collective-permute-start | bytes 1572872 | tf_op jit(solution)/shard_map/ppermute | solution.py:41
  65.8 8.9 %collective-permute-start.19 = (bf16[256,1024]{1,0:T(8,128)(2,1)S(1)}, bf16[256,1024]{1,0:T(8,128)(2,1)S(1)}, u32[]{:S(2)}, u32[]{:S(2)}) collective-permute-start(bf16[256,1024]{1,0:T(8,128)(2,1)S(1)} %collective-permute-done.14.refs_10_), channel_id=1, source_target_pairs={{0,1},{1,0},{2,3},{3,2},{4,5},{5,4},{6,7},{7,6},{8,9},{9,8},{10,11... | collective-permute-start | bytes 1572872 | tf_op jit(solution)/shard_map/ppermute | solution.py:41
  66.3 6.9 %collective-permute-start.16 = (bf16[4,64,384]{2,1,0:T(8,128)(2,1)S(1)}, bf16[4,64,384]{2,1,0:T(8,128)(2,1)S(1)}, u32[]{:S(2)}, u32[]{:S(2)}) collective-permute-start(bf16[4,64,384]{2,1,0:T(8,128)(2,1)S(1)} %gather_heads.1.refs_4_), channel_id=1, source_target_pairs={{0,2},{1,3},{2,0},{3,1},{4,6},{5,7},{6,4},{7,5},{8,10},{9,11},{10,... | collective-permute-start | bytes 589832 | tf_op jit(solution)/shard_map/ppermute | solution.py:41
  67.4 5.8 %collective-permute-start.15 = (bf16[4,64,384]{2,1,0:T(8,128)(2,1)S(1)}, bf16[4,64,384]{2,1,0:T(8,128)(2,1)S(1)}, u32[]{:S(2)}, u32[]{:S(2)}) collective-permute-start(bf16[4,64,384]{2,1,0:T(8,128)(2,1)S(1)} %gather_heads.1.refs_4_), channel_id=1, source_target_pairs={{0,1},{1,0},{2,3},{3,2},{4,5},{5,4},{6,7},{7,6},{8,9},{9,8},{10,11... | collective-permute-start | bytes 589832 | tf_op jit(solution)/shard_map/ppermute | solution.py:41
  73.2 1.4 %collective-permute-start.17 = (bf16[4,64,384]{2,1,0:T(8,128)(2,1)S(1)}, bf16[4,64,384]{2,1,0:T(8,128)(2,1)S(1)}, u32[]{:S(2)}, u32[]{:S(2)}) collective-permute-start(bf16[4,64,384]{2,1,0:T(8,128)(2,1)S(1)} %collective-permute-done.16.refs_6_), channel_id=1, source_target_pairs={{0,1},{1,0},{2,3},{3,2},{4,5},{5,4},{6,7},{7,6},{8,9},{9,8},{10,11... | collective-permute-start | bytes 589832 | tf_op jit(solution)/shard_map/ppermute | solution.py:41
  78.2 1.5 %collective-permute-start.21 = (bf16[384,256]{1,0:T(8,128)(2,1)S(1)}, bf16[384,256]{1,0:T(8,128)(2,1)S(1)}, u32[]{:S(2)}, u32[]{:S(2)}) collective-permute-start(bf16[384,256]{1,0:T(8,128)(2,1)S(1)} %get-tuple-element.68), channel_id=1, source_target_pairs={{0,1},{1,0},{2,3},{3,2},{4,5},{5,4},{6,7},{7,6},{8,9},{9,8},{10,11... | collective-permute-start | bytes 589832 | tf_op jit(solution)/shard_map/ppermute | solution.py:41
  78.4 2.6 %collective-permute-start.20 = (bf16[384,256]{1,0:T(8,128)(2,1)S(1)}, bf16[384,256]{1,0:T(8,128)(2,1)S(1)}, u32[]{:S(2)}, u32[]{:S(2)}) collective-permute-start(bf16[384,256]{1,0:T(8,128)(2,1)S(1)} %get-tuple-element.66), channel_id=1, source_target_pairs={{0,1},{1,0},{2,3},{3,2},{4,5},{5,4},{6,7},{7,6},{8,9},{9,8},{10,11... | collective-permute-start | bytes 589832 | tf_op jit(solution)/shard_map/ppermute | solution.py:41
  79.7 7.0 %collective-permute-start.22 = (bf16[384,256]{1,0:T(8,128)(2,1)S(1)}, bf16[384,256]{1,0:T(8,128)(2,1)S(1)}, u32[]{:S(2)}, u32[]{:S(2)}) collective-permute-start(bf16[384,256]{1,0:T(8,128)(2,1)S(1)} %add_convert_fusion.1), channel_id=1, source_target_pairs={{0,2},{1,3},{2,0},{3,1},{4,6},{5,7},{6,4},{7,5},{8,10},{9,11},{10,... | collective-permute-start | bytes 589832 | tf_op jit(solution)/shard_map/ppermute | solution.py:41
